TPU v7x, 128 devices: a whole 4x4x4 slice. The times are simulated.
128 devices in a mesh: row: 8 (over z, y_lo), col: 16 (over x, y_hi, core).
Axes of the slice: x: 4, y: 4 (y_hi: 2, y_lo: 2; y = y_hi * 2 + y_lo), z: 4, core: 2. Of those that a mesh axis runs over, the one named last changes fastest.
Arguments:
- factor_panel: float32 [16384, 512], P(('row', 'col')), may hold values from -0.6 to 0.6
- pivot_inverse: float32 [512, 512], replicated, may hold values from -3 to 3
- ancestor_inverse: float32 [16384, 16384], P('row', 'col'), may hold values from -0.046875 to 0.046875
- diag_inverse: float32 [512, 512], replicated, may hold values from -6 to 6
- block_map: int32 [128], replicated, may hold values from 0 to 127, as said below
Outputs:
- offdiag_block: float32 [16384, 512], P(('row', 'col'))
- diag_block: float32 [512, 512], replicated
Inputs may be any that keep to these rules, and one draw needn't show every extreme that they name: block_map is a permutation of the blocks that maps every aligned group of 16 blocks onto itself.
All inputs are finite; a program needn't handle non-finite values.
Results may differ from a plain program's by a relative error of at most 0.000071.
Values sent between devices are 32-bit elements; how exact they have to be, the bound alone decides.
No kernel may reach another device: no remote copies, remote signals or barrier semaphores. Data moves between devices by JAX's collectives and lax.ppermute only.
A program may use at most 128 MiB of HBM per device.

v0:
```python
import jax
import jax.numpy as jnp
from jax import lax
from jax.sharding import PartitionSpec as P

BLOCK = 128


def invert_map(local_map, count):
    positions = jnp.arange(count, dtype=jnp.int32)
    return jnp.sum(
        jnp.where(local_map[None, :] == positions[:, None], positions[None, :], 0), axis=1
    )


def reduce_partials(partial_value):
    return -lax.psum_scatter(partial_value, "col", scatter_dimension=0, tiled=True)


def shards(factor_panel, pivot_inverse, ancestor_inverse, diag_inverse, block_map):
    highest = lax.Precision.HIGHEST
    normed = jnp.dot(
        factor_panel, pivot_inverse, precision=highest, preferred_element_type=jnp.float32
    )
    rows_local, panel_width = normed.shape
    row_span = ancestor_inverse.shape[0]
    col_span = ancestor_inverse.shape[1]
    total_blocks = block_map.shape[0]
    row_blocks = row_span // BLOCK
    col_blocks = col_span // BLOCK
    my_row = lax.axis_index("row")
    my_col = lax.axis_index("col")
    everything = lax.all_gather(normed, ("row", "col"), axis=0, tiled=True)
    source = invert_map(block_map, total_blocks)
    blocks_all = everything.reshape(total_blocks, BLOCK, panel_width)
    pick_rows = lax.dynamic_slice_in_dim(source, my_row * row_blocks, row_blocks)
    anc_rows = jnp.take(blocks_all, pick_rows, axis=0).reshape(row_span, panel_width)
    pick_cols = lax.dynamic_slice_in_dim(source, my_col * col_blocks, col_blocks)
    anc_cols = jnp.take(blocks_all, pick_cols, axis=0).reshape(col_span, panel_width)
    partial_value = jnp.dot(
        ancestor_inverse, anc_cols, precision=highest, preferred_element_type=jnp.float32
    )
    offdiag_block = reduce_partials(partial_value)
    own_panel = lax.dynamic_slice_in_dim(anc_rows, my_col * rows_local, rows_local, 0)
    diag_term = lax.dot_general(
        own_panel,
        offdiag_block,
        (((0,), (0,)), ((), ())),
        precision=highest,
        preferred_element_type=jnp.float32,
    )
    diag_block = diag_inverse - lax.psum(diag_term, ("row", "col"))
    return (offdiag_block, diag_block)


def solution(mesh):
    placed = (P(("row", "col"), None), P(), P("row", "col"), P(), P())
    return jax.shard_map(
        shards,
        mesh=mesh,
        in_specs=placed,
        out_specs=(P(("row", "col"), None), P()),
        check_vma=False,
    )
```

profile of v0, /device:TPU:1, one launch (start us, length us, event | category | flops | bytes accessed | tf_op | source)
XLA Modules:
  0.0 521.9 jit_solution(2371681334984736671)
XLA Ops:
  7.2 0.0 copy-start
  7.2 0.0 all-gather.2.cloned.1.call-start
  7.2 1.2 copy-done
  8.4 2.4 fusion.6
  10.8 0.0 all-gather.2.cloned.1.call-update
  10.8 0.0 reduce-scatter.2.cloned.1.call-start
  10.8 0.8 select_reduce_fusion
  11.6 0.1 compare_and_fusion.1
  11.7 0.1 broadcast_bitcast_fusion.1
  11.8 235.7 %all-gather.2.cloned.1.call-done = f32[16384,512]{1,0:T(8,128)} async-done(((f32[128,512]{1,0:T(8,128)}), f32[16384,512]{1,0:T(8,128)}) %all-gather.2.cloned.1.call-update) | async-done | bytes 33554448 | tf_op jit(solution)/shard_map/all_gather | solution.py:33
  247.4 2.2 gather_fusion
  249.6 0.2 bitcast_select_fusion
  249.8 30.8 %convolution_bitcast_fusion = f32[2048,512]{0,1:T(8,128)} fusion(f32[1024,512]{1,0:T(8,128)S(1)} %bitcast_select_fusion, f32[2048,1024]{1,0:T(8,128)} %param.7), kind=kOutput, calls=%fused_computation.2 | convolution fusion | flops 12884901888 | bytes 14680064 | tf_op jit(solution)/shard_map/dot_general | solution.py:40
  280.6 0.0 reduce-scatter.2.cloned.1.call-update
  280.6 0.0 all-reduce.2.cloned.1.call-start
  280.7 0.1 compare_and_fusion
  280.8 0.1 broadcast_bitcast_fusion
  280.9 0.1 dynamic-slice
  280.9 0.0 copy-start.1
  281.0 4.9 gather_fusion.1
  285.9 73.2 %reduce-scatter.2.cloned.1.call-done = f32[128,512]{0,1:T(8,128)} async-done(((f32[2048,512]{0,1:T(8,128)}), f32[128,512]{0,1:T(8,128)}) %reduce-scatter.2.cloned.1.call-update) | async-done | bytes 262160 | tf_op jit(solution)/shard_map/reduce_scatter | solution.py:17
  359.0 3.1 fusion
  362.1 0.0 all-reduce.2.cloned.1.call-update
  362.1 1.0 neg.3
  363.1 0.8 copy.8
  363.9 149.0 %all-reduce.2.cloned.1.call-done = f32[512,512]{1,0:T(8,128)} async-done(((f32[512,512]{1,0:T(8,128)}), f32[512,512]{1,0:T(8,128)}) %all-reduce.2.cloned.1.call-update) | async-done | bytes 1048592 | tf_op jit(solution)/shard_map/psum | solution.py:52
  513.0 0.0 copy-done.1
  513.0 2.4 sub.3
  (2 shorter events, 0.0 us)
Async XLA Ops:
  7.2 1.2 copy-start
  7.2 240.3 %all-gather.2.cloned.1.call-start = ((), (), s32[]{:S(2)}) async-start(), calls=%async_computation.1 | async-start | bytes 33816576 | tf_op jit(solution)/shard_map/all_gather | solution.py:33
  10.8 348.2 %reduce-scatter.2.cloned.1.call-start = ((), (), s32[]{:S(2)}) async-start(), calls=%async_computation.2 | async-start | bytes 4456448 | tf_op jit(solution)/shard_map/reduce_scatter | solution.py:17
  280.6 232.3 %all-reduce.2.cloned.1.call-start = ((), (), s32[]{:S(2)}) async-start(), calls=%async_computation.3 | async-start | bytes 2097152 | tf_op jit(solution)/shard_map/psum | solution.py:52
  280.9 232.0 %copy-start.1 = (f32[512,512]{1,0:T(8,128)S(1)}, f32[512,512]{1,0:T(8,128)}, u32[]{:S(2)}) copy-start(f32[512,512]{1,0:T(8,128)} %param.8) | copy-start | bytes 3145732
Sparse Core Ops, SparseCore 0:
  10.9 236.4 all-gather.1
  280.8 78.1 reduce-scatter.1
  364.4 148.5 all-reduce.1
where the time goes:
time: 522 us
  waiting for transfers between devices  458 us (88%)
  matrix products  36.2 us (7%)
  between operations  13.8 us (3%)
  local copies, waits for them, and re-layouts  9.33 us (2%)
    all_gather x1, waiting for transfers between devices, shards(): everything = lax.all_gather(normed, ('row', 'col'), axis=0, tiled=True)  236 us
    psum x1, waiting for transfers between devices, shards(): diag_block = diag_inverse - lax.psum(diag_term, ('row', 'col'))  149 us
    reduce_scatter x1, waiting for transfers between devices, reduce_partials(): lax.psum_scatter(partial_value, 'col', scatter_dimension=0, tiled=True)  73.2 us
    dot_general x1, matrix products, shards(): jnp.dot(ancestor_inverse, anc_cols, precision=highest, preferred_element_...  30.8 us
  transfers between devices with their start and end apart: 3, of which 3 were waited for; matrix products, arithmetic and copies ran while one was open for 2% of the time, Pallas kernels for 0%

commit v1 on v0

v1 whole, which is shorter than its diff:
```python
import jax
import jax.numpy as jnp
from jax import lax
from jax.sharding import Mesh, PartitionSpec as P

BLOCK = 128
ROW = ("z", "yl")
CHIPS_COL = ("x", "yh")
ALL = ("z", "yl", "x", "yh", "c")
CHIPS = ("z", "yl", "x", "yh")
HIGH = lax.Precision.HIGH

SWAP = [(0, 1), (1, 0)]
TO_COLUMN = [(g * 16 + j, (j // 2) * 16 + 2 * g + j % 2) for g in range(8) for j in range(16)]
TO_OWNER = [(r * 16 + 2 * g + h, g * 16 + 8 * h + r) for r in range(8) for g in range(8) for h in range(2)]


def dot(a, b):
    return jnp.dot(a, b, precision=HIGH, preferred_element_type=jnp.float32)


def invert_map(local_map, count):
    positions = jnp.arange(count, dtype=jnp.int32)
    return jnp.sum(
        jnp.where(local_map[None, :] == positions[:, None], positions[None, :], 0), axis=1
    )


def spread(value, axes, count):
    copies = jnp.broadcast_to(value[None], (count,) + value.shape)
    return lax.all_to_all(copies, axes, 0, 0, tiled=True)


def shards(factor_panel, pivot_inverse, ancestor_inverse, diag_inverse, block_map):
    width = factor_panel.shape[1]
    core = lax.axis_index("c")
    my_row = lax.axis_index(ROW)
    group = lax.axis_index(CHIPS_COL)

    normed = dot(factor_panel, pivot_inverse)
    column_block = lax.ppermute(normed, ALL, TO_COLUMN)
    mine = spread(column_block, ROW, 8)
    other = lax.ppermute(mine, "c", SWAP)
    sources = jnp.concatenate([mine, other], axis=0)

    source = invert_map(block_map, block_map.shape[0])
    picks = lax.dynamic_slice_in_dim(source, group * 16 + core * 8, 8) - group * 16
    slots = picks // 2 + 8 * (picks % 2 != core)
    anc_blocks = jnp.take(sources, slots, axis=0)
    anc_cols = anc_blocks.reshape(8 * BLOCK, width)
    own_panel = lax.ppermute(
        lax.dynamic_index_in_dim(anc_blocks, my_row, 0, keepdims=False), ALL, TO_OWNER
    )

    partial_value = dot(ancestor_inverse, anc_cols).reshape(8, 2, BLOCK, width)
    keep = lax.dynamic_index_in_dim(partial_value, core, 1, keepdims=False)
    give = lax.dynamic_index_in_dim(partial_value, 1 - core, 1, keepdims=False)
    chip_sum = keep + lax.ppermute(give, "c", SWAP)
    parts = lax.all_to_all(chip_sum, CHIPS_COL, 0, 0, tiled=True)
    offdiag_block = -jnp.sum(parts, axis=0)

    term = lax.dot_general(
        own_panel,
        offdiag_block,
        (((0,), (0,)), ((), ())),
        precision=HIGH,
        preferred_element_type=jnp.float32,
    )
    half = width // 2
    keep_term = lax.dynamic_slice_in_dim(term, core * half, half, 0)
    give_term = lax.dynamic_slice_in_dim(term, (1 - core) * half, half, 0)
    term = keep_term + lax.ppermute(give_term, "c", SWAP)
    pieces = lax.all_to_all(term.reshape(64, half // 64, width), CHIPS, 0, 0, tiled=True)
    piece = jnp.sum(pieces, axis=0)
    mine_half = spread(piece, CHIPS, 64).reshape(half, width)
    other_half = lax.ppermute(mine_half, "c", SWAP)
    low = jnp.where(core == 0, mine_half, other_half)
    high = jnp.where(core == 0, other_half, mine_half)
    diag_block = diag_inverse - jnp.concatenate([low, high], axis=0)
    return (offdiag_block, diag_block)


def solution(mesh):
    fine = Mesh(mesh.devices.reshape(4, 2, 4, 2, 2), ALL)
    rows, cols = ROW, ("x", "yh", "c")
    placed = (P(ALL, None), P(), P(rows, cols), P(), P())
    return jax.shard_map(
        shards,
        mesh=fine,
        in_specs=placed,
        out_specs=(P(ALL, None), P()),
        check_vma=False,
    )
```

time: 522 us -> 215 us (0.41)
  waiting for transfers between devices: 458 us -> 33.8 us
  blocking collectives: 0 us -> 104 us
  starting transfers between devices: 0.12 us -> 23.9 us
  matrix products: 36.2 us -> 19.4 us
  between operations: 13.8 us -> 0.82 us
  local copies, waits for them, and re-layouts: 9.33 us -> 21.1 us
  other arithmetic: 4.53 us -> 11.4 us
    all_gather x1 -> x0, waiting for transfers between devices: 236 us -> none  [shards(): everything = lax.all_gather(normed, ('row', 'col'), axis=0, tiled=True)]
    psum x1 -> x0, waiting for transfers between devices: 149 us -> none  [shards(): diag_block = diag_inverse - lax.psum(diag_term, ('row', 'col'))]
    all_to_all x0 -> x3, blocking collectives: none -> 104 us  [the longest x2 69.3 us: spread(): return lax.all_to_all(copies, axes, 0, 0, tiled=True)]
    reduce_scatter x1 -> x0, waiting for transfers between devices: 73.2 us -> none  [reduce_partials(): lax.psum_scatter(partial_value, 'col', scatter_dimension=0, tiled=True)]
    all_to_all x0 -> x1, waiting for transfers between devices: none -> 24.1 us  [shards(): parts = lax.all_to_all(chip_sum, CHIPS_COL, 0, 0, tiled=True)]
    ppermute x0 -> x6, starting transfers between devices: none -> 14.3 us  [the longest x1 5.69 us: shards(): lax.ppermute(lax.dynamic_index_in_dim(anc_blocks, my_row, 0, keepdims=Fal...]
    dot_general x2, matrix products: 33.1 us -> 18.8 us  [dot(): return jnp.dot(a, b, precision=HIGH, preferred_element_type=jnp.float32)]
    ppermute x0 -> x6, waiting for transfers between devices: none -> 9.75 us  [the longest x1 3.79 us: shards(): chip_sum = keep + lax.ppermute(give, 'c', SWAP)]
  transfers between devices with their start and end apart: 3 -> 7, of which waited for: 3 -> 5; matrix products, arithmetic and copies ran while one was open for 2% -> 2% of each run, Pallas kernels for 0% -> 0%
where the time goes in v1:
time: 215 us; the launch traced here: 214 us
  blocking collectives  104 us (48%)
  waiting for transfers between devices  33.8 us (16%)
  starting transfers between devices  23.9 us (11%)
  local copies, waits for them, and re-layouts  21.1 us (10%)
  matrix products  19.4 us (9%)
  other arithmetic  11.4 us (5%)
    all_to_all x2, blocking collectives, spread(): return lax.all_to_all(copies, axes, 0, 0, tiled=True)  69.3 us
    all_to_all x1, blocking collectives, shards(): lax.all_to_all(term.reshape(64, half // 64, width), CHIPS, 0, 0, tiled=True)  34.8 us
    all_to_all x1, waiting for transfers between devices, shards(): parts = lax.all_to_all(chip_sum, CHIPS_COL, 0, 0, tiled=True)  24.1 us
    dot_general x2, matrix products, dot(): return jnp.dot(a, b, precision=HIGH, preferred_element_type=jnp.float32)  18.8 us
    all_to_all x1, starting transfers between devices, shards(): parts = lax.all_to_all(chip_sum, CHIPS_COL, 0, 0, tiled=True)  9.54 us
    dynamic_slice x1, local copies, waits for them, and re-layouts, shards(): keep = lax.dynamic_index_in_dim(partial_value, core, 1, keepdims=False)  7.78 us
    reshape x1, local copies, waits for them, and re-layouts, shards(): partial_value = dot(ancestor_inverse, anc_cols).reshape(8, 2, BLOCK, width)  6.61 us
    ppermute x1, starting transfers between devices, shards(): lax.ppermute(lax.dynamic_index_in_dim(anc_blocks, my_row, 0, keepdims=Fal...  5.69 us
  transfers between devices with their start and end apart: 7, of which 5 were waited for; matrix products, arithmetic and copies ran while one was open for 2% of the time, Pallas kernels for 0%

profile of v1, /device:TPU:1, one launch (start us, length us, event | category | flops | bytes accessed | tf_op | source)
XLA Modules:
  0.0 214.5 jit_solution(5984512575159541367)
XLA Ops:
  0.6 1.2 copy-done
  1.9 1.4 fusion.4
  3.2 0.7 collective-permute-start
  3.9 0.3 broadcast_in_dim.52
  4.2 53.7 %all_to_all.20 = f32[8,128,512]{2,1,0:T(8,128)S(1)} all-to-all(f32[8,128,512]{2,1,0:T(8,128)S(1)} %broadcast_in_dim.52), channel_id=1, replica_groups=mesh['z'=4,'yl'=2,'x'=4,'yh'=2,'c'=2] {'z','yl'}, dimensions={0} | all-to-all | bytes 4194304 | tf_op jit(solution)/shard_map/all_to_all | solution.py:31
  57.9 2.7 %collective-permute-start.1 = (f32[8,128,512]{2,1,0:T(8,128)S(1)}, f32[8,128,512]{2,1,0:T(8,128)}, u32[]{:S(2)}, u32[]{:S(2)}) collective-permute-start(f32[8,128,512]{2,1,0:T(8,128)S(1)} %all_to_all.20), channel_id=1, source_target_pairs={{0,1},{1,0},{2,3},{3,2},{4,5},{5,4},{6,7},{7,6},{8,9},{9,8},{10,11... | collective-permute-start | bytes 6291464 | tf_op jit(solution)/shard_map/ppermute | solution.py:43
  60.8 3.6 %collective-permute-done.1 = f32[8,128,512]{2,1,0:T(8,128)} collective-permute-done((f32[8,128,512]{2,1,0:T(8,128)S(1)}, f32[8,128,512]{2,1,0:T(8,128)}, u32[]{:S(2)}, u32[]{:S(2)}) %collective-permute-start.1) | collective-permute-done | bytes 2097184 | tf_op jit(solution)/shard_map/ppermute | solution.py:43
  64.4 4.3 %pad_maximum_fusion = f32[16,128,512]{2,1,0:T(8,128)} fusion(f32[8,128,512]{2,1,0:T(8,128)} %collective-permute-done.1, f32[8,128,512]{2,1,0:T(8,128)S(1)} %all_to_all.20), kind=kLoop, calls=%fused_computation.1 | loop fusion | flops 1048576 | bytes 8388608 | tf_op jit(solution)/shard_map/concatenate | solution.py:44
  68.7 2.9 %gather_fusion = f32[8,128,512]{2,1,0:T(8,128)S(1)} fusion(f32[16,128,512]{2,1,0:T(8,128)} %pad_maximum_fusion, s32[1024]{0:T(1024)S(1)} %pad_clamp_fusion), kind=kCustom, calls=%fused_computation | custom fusion | bytes 4194336 | tf_op jit(solution)/shard_map/jit(_take)/gather | solution.py:49
  71.8 17.5 %convolution_bitcast_fusion = f32[2048,512]{0,1:T(8,128)} fusion(f32[1024,512]{1,0:T(8,128)S(1)} %bitcast_select_fusion, f32[2048,1024]{1,0:T(8,128)} %param.7), kind=kOutput, calls=%fused_computation.2 | convolution fusion | flops 6442450944 | bytes 14680064 | tf_op jit(solution)/shard_map/dot_general | solution.py:19
  89.3 6.6 %reshape.24 = f32[8,2,128,512]{2,1,0,3:T(2,128)} reshape(f32[2048,512]{0,1:T(8,128)} %convolution_bitcast_fusion) | data formatting | bytes 8388608 | tf_op jit(solution)/shard_map/reshape | solution.py:55
  95.9 7.8 %constant_dynamic-slice_fusion.1 = (f32[8,1,128,512]{2,1,0,3:T(1,128)S(1)}, f32[8,1,128,512]{2,1,0,3:T(1,128)S(1)}) fusion(f32[8,2,128,512]{2,1,0,3:T(2,128)} %reshape.24, s32[]{:T(128)S(6)} %select_n.65, s32[]{:T(128)S(6)} %select_n.66), kind=kLoop, calls=%fused_computation.22 | loop fusion | bytes 8388616 | tf_op jit(solution)/shard_map/jit(dynamic_index_in_dim)/dynamic_slice | solution.py:56
  103.7 0.4 copy.18
  104.1 0.5 collective-permute-start.2
  104.6 3.8 %collective-permute-done.2 = f32[8,128,512]{1,2,0:T(8,128)S(1)} collective-permute-done((f32[8,128,512]{1,2,0:T(8,128)S(1)}, f32[8,128,512]{1,2,0:T(8,128)S(1)}, u32[]{:S(2)}, u32[]{:S(2)}) %collective-permute-start.2) | collective-permute-done | bytes 2097184 | tf_op jit(solution)/shard_map/ppermute | solution.py:58
  108.3 1.7 bitcast_add_fusion
  110.1 9.5 %all-to-all-start.1 = ((f32[8,128,512]{1,2,0:T(8,128)}), f32[8,128,512]{1,2,0:T(8,128)}, u32[]{:S(2)}, u32[]{:S(2)}) async-start(f32[8,128,512]{1,2,0:T(8,128)} %bitcast_add_fusion), calls=%async_computation.1 | async-start | bytes 4194304 | tf_op jit(solution)/shard_map/all_to_all | solution.py:59
  119.6 0.6 dynamic-slice
  120.2 0.7 fusion
  120.9 5.7 %collective-permute-start.3 = (f32[128,512]{1,0:T(8,128)S(1)}, f32[128,512]{1,0:T(8,128)S(1)}, u32[]{:S(2)}, u32[]{:S(2)}) collective-permute-start(f32[128,512]{1,0:T(8,128)S(1)} %fusion), channel_id=1, source_target_pairs={{0,0},{1,8},{2,16},{3,24},{4,32},{5,40},{6,48},{7,56},{8,64},{9,72... | collective-permute-start | bytes 786440 | tf_op jit(solution)/shard_map/ppermute | solution.py:51
  126.6 24.1 %all-to-all-done.1 = f32[8,128,512]{1,2,0:T(8,128)} async-done(((f32[8,128,512]{1,2,0:T(8,128)}), f32[8,128,512]{1,2,0:T(8,128)}, u32[]{:S(2)}, u32[]{:S(2)}) %all-to-all-start.1) | async-done | bytes 2097184 | tf_op jit(solution)/shard_map/all_to_all | solution.py:59
  150.7 1.7 reduce_sum.28
  152.4 0.6 fusion.2
  153.1 1.5 collective-permute-start.4
  154.6 1.5 collective-permute-done.4
  156.4 34.8 %all_to_all.21 = f32[64,4,512]{2,1,0:T(4,128)S(1)} all-to-all(f32[64,4,512]{2,1,0:T(4,128)S(1)} %reshape.25), channel_id=1, replica_groups=mesh['z'=4,'yl'=2,'x'=4,'yh'=2,'c'=2] {'z','yl','x','yh'}, dimensions={0} | all-to-all | bytes 1048576 | tf_op jit(solution)/shard_map/all_to_all | solution.py:73
  191.3 15.6 %all_to_all.22 = f32[64,4,512]{2,1,0:T(4,128)S(1)} all-to-all(f32[64,4,512]{2,1,0:T(4,128)S(1)} %broadcast_in_dim.57), channel_id=1, replica_groups=mesh['z'=4,'yl'=2,'x'=4,'yh'=2,'c'=2] {'z','yl','x','yh'}, dimensions={0} | all-to-all | bytes 1048576 | tf_op jit(solution)/shard_map/all_to_all | solution.py:31
  207.1 3.3 %collective-permute-start.5 = (f32[256,512]{1,0:T(8,128)S(1)}, f32[256,512]{1,0:T(8,128)}, u32[]{:S(2)}, u32[]{:S(2)}) collective-permute-start(f32[256,512]{1,0:T(8,128)S(1)} %reshape.26), channel_id=1, source_target_pairs={{0,1},{1,0},{2,3},{3,2},{4,5},{5,4},{6,7},{7,6},{8,9},{9,8},{10,11... | collective-permute-start | bytes 1572872 | tf_op jit(solution)/shard_map/ppermute | solution.py:76
  210.5 0.8 copy.14
  211.3 0.8 collective-permute-done.5
  212.1 1.1 broadcast_select_fusion.1
  213.3 1.2 maximum_subtract_fusion
  (19 shorter events, 1.2 us)
Async XLA Ops:
  0.6 1.2 copy-start
  3.2 0.7 collective-permute-start
  4.2 56.3 %copy-start.2 = (s32[128]{0:T(128)S(1)}, s32[128]{0:T(128)}, u32[]{:S(2)}) copy-start(s32[128]{0:T(128)} %param.9) | copy-start | bytes 1540
  57.9 6.6 %collective-permute-start.1 = (f32[8,128,512]{2,1,0:T(8,128)S(1)}, f32[8,128,512]{2,1,0:T(8,128)}, u32[]{:S(2)}, u32[]{:S(2)}) collective-permute-start(f32[8,128,512]{2,1,0:T(8,128)S(1)} %all_to_all.20), channel_id=1, source_target_pairs={{0,1},{1,0},{2,3},{3,2},{4,5},{5,4},{6,7},{7,6},{8,9},{9,8},{10,11... | collective-permute-start | bytes 6291464 | tf_op jit(solution)/shard_map/ppermute | solution.py:43
  104.1 4.2 %collective-permute-start.2 = (f32[8,128,512]{1,2,0:T(8,128)S(1)}, f32[8,128,512]{1,2,0:T(8,128)S(1)}, u32[]{:S(2)}, u32[]{:S(2)}) collective-permute-start(f32[8,128,512]{1,2,0:T(8,128)S(1)} %bitcast.20), channel_id=1, source_target_pairs={{0,1},{1,0},{2,3},{3,2},{4,5},{5,4},{6,7},{7,6},{8,9},{9,8},{10,11... | collective-permute-start | bytes 6291464 | tf_op jit(solution)/shard_map/ppermute | solution.py:58
  110.1 40.6 %all-to-all-start.1 = ((f32[8,128,512]{1,2,0:T(8,128)}), f32[8,128,512]{1,2,0:T(8,128)}, u32[]{:S(2)}, u32[]{:S(2)}) async-start(f32[8,128,512]{1,2,0:T(8,128)} %bitcast_add_fusion), calls=%async_computation.1 | async-start | bytes 4194304 | tf_op jit(solution)/shard_map/all_to_all | solution.py:59
  120.9 31.5 %collective-permute-start.3 = (f32[128,512]{1,0:T(8,128)S(1)}, f32[128,512]{1,0:T(8,128)S(1)}, u32[]{:S(2)}, u32[]{:S(2)}) collective-permute-start(f32[128,512]{1,0:T(8,128)S(1)} %fusion), channel_id=1, source_target_pairs={{0,0},{1,8},{2,16},{3,24},{4,32},{5,40},{6,48},{7,56},{8,64},{9,72... | collective-permute-start | bytes 786440 | tf_op jit(solution)/shard_map/ppermute | solution.py:51
  153.1 3.0 %collective-permute-start.4 = (f32[256,512]{1,0:T(8,128)S(1)}, f32[256,512]{1,0:T(8,128)S(1)}, u32[]{:S(2)}, u32[]{:S(2)}) collective-permute-start(f32[256,512]{1,0:T(8,128)S(1)} %constant_dynamic-slice_fusion.2), channel_id=1, source_target_pairs={{0,1},{1,0},{2,3},{3,2},{4,5},{5,4},{6,7},{7,6},{8,9},{9,8},{10,11... | collective-permute-start | bytes 1572872 | tf_op jit(solution)/shard_map/ppermute | solution.py:72
  206.9 6.3 %copy-start.1 = (f32[512,512]{1,0:T(8,128)S(1)}, f32[512,512]{1,0:T(8,128)}, u32[]{:S(2)}) copy-start(f32[512,512]{1,0:T(8,128)} %param.8) | copy-start | bytes 3145732
  207.1 5.0 %collective-permute-start.5 = (f32[256,512]{1,0:T(8,128)S(1)}, f32[256,512]{1,0:T(8,128)}, u32[]{:S(2)}, u32[]{:S(2)}) collective-permute-start(f32[256,512]{1,0:T(8,128)S(1)} %reshape.26), channel_id=1, source_target_pairs={{0,1},{1,0},{2,3},{3,2},{4,5},{5,4},{6,7},{7,6},{8,9},{9,8},{10,11... | collective-permute-start | bytes 1572872 | tf_op jit(solution)/shard_map/ppermute | solution.py:76

commit v2 on v1

v2 whole, which is shorter than its diff:
```python
import jax
import jax.numpy as jnp
from jax import lax
from jax.experimental import pallas as pl
from jax.experimental.pallas import tpu as pltpu
from jax.sharding import Mesh, PartitionSpec as P

BLOCK = 128
ROW = ("z", "yl")
CHIPS_COL = ("x", "yh")
ALL = ("z", "yl", "x", "yh", "c")
CHIPS = ("z", "yl", "x", "yh")
HIGH = lax.Precision.HIGH
SWAP = [(0, 1), (1, 0)]
TILE = 2


def flat(z, yl, x, yh, c):
    return (z * 2 + yl) * 16 + x * 4 + yh * 2 + c


DEVICES = [
    (z, yl, x, yh, c)
    for z in range(4)
    for yl in range(2)
    for x in range(4)
    for yh in range(2)
    for c in range(2)
]
TO_COLUMN = [
    (flat(z, yl, x, yh, c), flat(x, yh ^ (x & 1), z, yl, c)) for z, yl, x, yh, c in DEVICES
]
TO_OWNER = [
    (flat(z, yl, x, yh, c), flat(x, yh, 2 * c + (z >> 1), yl ^ (z & 1), z & 1))
    for z, yl, x, yh, c in DEVICES
]


def dot(a, b):
    return jnp.dot(a, b, precision=HIGH, preferred_element_type=jnp.float32)


def invert_map(local_map, count):
    positions = jnp.arange(count, dtype=jnp.int32)
    return jnp.sum(
        jnp.where(local_map[None, :] == positions[:, None], positions[None, :], 0), axis=1
    )


def spread(value, axes, count):
    copies = jnp.broadcast_to(value[None], (count,) + value.shape)
    return lax.all_to_all(copies, axes, 0, 0, tiled=True)


def split(value):
    high = value.astype(jnp.bfloat16)
    low = (value - high.astype(jnp.float32)).astype(jnp.bfloat16)
    return high, low


def half_kernel(table, a_ref, mine_ref, other_ref, out_ref, high_ref, low_ref):
    @pl.when(pl.program_id(0) == 0)
    def _():
        for t in range(8):
            slot = table[t]
            own = mine_ref[slot & 7]
            far = other_ref[slot & 7]
            high, low = split(jnp.where(slot < 8, own, far))
            high_ref[pl.ds(t * BLOCK, BLOCK), :] = high
            low_ref[pl.ds(t * BLOCK, BLOCK), :] = low

    rows = TILE * BLOCK
    a_high, a_low = split(a_ref[...].reshape(rows, a_ref.shape[-1]))
    total = jnp.dot(a_high, low_ref[...], preferred_element_type=jnp.float32)
    total += jnp.dot(a_low, high_ref[...], preferred_element_type=jnp.float32)
    total += jnp.dot(a_high, high_ref[...], preferred_element_type=jnp.float32)
    out_ref[...] = total.reshape(out_ref.shape)


def half_product(table, ancestor, mine, other):
    depth = ancestor.shape[-1]
    width = mine.shape[-1]
    whole = pl.BlockSpec((8, BLOCK, width), lambda i, table: (0, 0, 0))
    return pl.pallas_call(
        half_kernel,
        grid_spec=pltpu.PrefetchScalarGridSpec(
            num_scalar_prefetch=1,
            grid=(8 // TILE,),
            in_specs=[
                pl.BlockSpec((TILE, 1, BLOCK, depth), lambda i, table: (i, table[8], 0, 0)),
                whole,
                whole,
            ],
            out_specs=pl.BlockSpec((TILE, BLOCK, width), lambda i, table: (i, 0, 0)),
            scratch_shapes=[
                pltpu.VMEM((depth, width), jnp.bfloat16),
                pltpu.VMEM((depth, width), jnp.bfloat16),
            ],
        ),
        out_shape=jax.ShapeDtypeStruct((8, BLOCK, width), jnp.float32),
        cost_estimate=pl.CostEstimate(
            flops=3 * 2 * 8 * BLOCK * depth * width,
            bytes_accessed=4 * (8 * BLOCK * depth + 3 * 8 * BLOCK * width),
            transcendentals=0,
        ),
    )(table, ancestor, mine, other)


def shards(factor_panel, pivot_inverse, ancestor_inverse, diag_inverse, block_map):
    width = factor_panel.shape[1]
    core = lax.axis_index("c")
    z, yl = lax.axis_index("z"), lax.axis_index("yl")
    group = lax.axis_index(CHIPS_COL)

    normed = dot(factor_panel, pivot_inverse)
    column_block = lax.ppermute(normed, ALL, TO_COLUMN)
    mine = spread(column_block, ROW, 8).reshape(8, BLOCK, width)
    other = lax.ppermute(mine, "c", SWAP)

    source = invert_map(block_map, block_map.shape[0])
    picks = lax.dynamic_slice_in_dim(source, group * 16 + core * 8, 8) - group * 16
    slots = 2 * (picks >> 2) + (((picks >> 1) ^ (picks >> 2)) & 1)
    slots = slots + 8 * ((picks & 1) != core)
    send = (z >> 1) * 4 + (yl ^ (z & 1)) * 2 + (z & 1)
    slot = lax.dynamic_index_in_dim(slots, send, 0, keepdims=False)
    own_panel = jnp.where(
        slot < 8,
        lax.dynamic_index_in_dim(mine, slot & 7, 0, keepdims=False),
        lax.dynamic_index_in_dim(other, slot & 7, 0, keepdims=False),
    )
    own_panel = lax.ppermute(own_panel, ALL, TO_OWNER)

    ancestor = ancestor_inverse.reshape(8, 2, BLOCK, ancestor_inverse.shape[1])
    tables = [jnp.concatenate([slots, c[None]]).astype(jnp.int32) for c in (1 - core, core)]
    give = half_product(tables[0], ancestor, mine, other)
    keep = half_product(tables[1], ancestor, mine, other)
    chip_sum = keep + lax.ppermute(give, "c", SWAP)
    parts = lax.all_to_all(chip_sum, CHIPS_COL, 0, 0, tiled=True)
    offdiag_block = -jnp.sum(parts, axis=0)

    term = lax.dot_general(
        own_panel,
        offdiag_block,
        (((0,), (0,)), ((), ())),
        precision=HIGH,
        preferred_element_type=jnp.float32,
    )
    half = width // 2
    keep_term = lax.dynamic_slice_in_dim(term, core * half, half, 0)
    give_term = lax.dynamic_slice_in_dim(term, (1 - core) * half, half, 0)
    term = keep_term + lax.ppermute(give_term, "c", SWAP)
    rows = half // 64
    pieces = lax.all_to_all(term.reshape(64, rows, width), CHIPS, 0, 0, tiled=True)
    first = core * half + lax.axis_index(CHIPS) * rows
    piece = lax.dynamic_slice_in_dim(diag_inverse, first, rows, 0) - jnp.sum(pieces, axis=0)
    mine_half = spread(piece, CHIPS, 64).reshape(half, width)
    other_half = lax.ppermute(mine_half, "c", SWAP)
    low = jnp.where(core == 0, mine_half, other_half)
    high = jnp.where(core == 0, other_half, mine_half)
    return (offdiag_block, jnp.concatenate([low, high], axis=0))


def solution(mesh):
    fine = Mesh(mesh.devices.reshape(4, 2, 4, 2, 2), ALL)
    rows, cols = ROW, ("x", "yh", "c")
    placed = (P(ALL, None), P(), P(rows, cols), P(), P())
    return jax.shard_map(
        shards,
        mesh=fine,
        in_specs=placed,
        out_specs=(P(ALL, None), P()),
        check_vma=False,
    )
```

time: 215 us -> 175 us (0.81)
  blocking collectives: 104 us -> 68.1 us
  Pallas kernels: 0 us -> 17.8 us
  local copies, waits for them, and re-layouts: 21.1 us -> 3.31 us
  matrix products: 19.4 us -> 2.93 us
  waiting for transfers between devices: 33.8 us -> 44.2 us
  starting transfers between devices: 23.9 us -> 27.5 us
  other arithmetic: 11.4 us -> 8.29 us
    all_to_all x1 -> x0, blocking collectives: 34.8 us -> none  [shards(): lax.all_to_all(term.reshape(64, half // 64, width), CHIPS, 0, 0, tiled=True)]
    pallas_call x0 -> x2, Pallas kernels: none -> 17.8 us  [half_product(): pl.pallas_call(half_kernel, grid_spec=pltpu.PrefetchScalarGridSpec(num_sc...]
    dot_general x2 -> x1, matrix products: 18.8 us -> 1.37 us  [dot(): return jnp.dot(a, b, precision=HIGH, preferred_element_type=jnp.float32)]
    all_to_all x0 -> x1, waiting for transfers between devices: none -> 12.4 us  [shards(): lax.all_to_all(term.reshape(64, rows, width), CHIPS, 0, 0, tiled=True)]
    all_to_all x0 -> x1, starting transfers between devices: none -> 11.2 us  [shards(): lax.all_to_all(term.reshape(64, rows, width), CHIPS, 0, 0, tiled=True)]
    dynamic_slice x3 -> x1, local copies, waits for them, and re-layouts: 8.77 us -> 0.58 us  [shards(): slot = lax.dynamic_index_in_dim(slots, send, 0, keepdims=False)]
    reshape x2 -> x1, local copies, waits for them, and re-layouts: 6.75 us -> 0.94 us  [shards(): term.reshape(64, rows, width)]
    all_to_all x1, starting transfers between devices: 9.54 us -> 4.59 us  [shards(): parts = lax.all_to_all(chip_sum, CHIPS_COL, 0, 0, tiled=True)]
  transfers between devices with their start and end apart: 7 -> 8, of which waited for: 5 -> 6; matrix products, arithmetic and copies ran while one was open for 2% -> 2% of each run, Pallas kernels for 0% -> 5%
where the time goes in v2:
time: 175 us; the launch traced here: 174 us
  blocking collectives  68.1 us (39%)
  waiting for transfers between devices  44.2 us (25%)
  starting transfers between devices  27.5 us (16%)
  Pallas kernels  17.8 us (10%)
  other arithmetic  8.29 us (5%)
  local copies, waits for them, and re-layouts  3.31 us (2%)
  matrix products  2.93 us (2%)
  between operations  2.1 us (1%)
    all_to_all x2, blocking collectives, spread(): return lax.all_to_all(copies, axes, 0, 0, tiled=True)  68.1 us
    all_to_all x1, waiting for transfers between devices, shards(): parts = lax.all_to_all(chip_sum, CHIPS_COL, 0, 0, tiled=True)  22.3 us
    pallas_call x2, Pallas kernels, half_product(): pl.pallas_call(half_kernel, grid_spec=pltpu.PrefetchScalarGridSpec(num_sc...  17.8 us
    all_to_all x1, waiting for transfers between devices, shards(): lax.all_to_all(term.reshape(64, rows, width), CHIPS, 0, 0, tiled=True)  12.4 us
    all_to_all x1, starting transfers between devices, shards(): lax.all_to_all(term.reshape(64, rows, width), CHIPS, 0, 0, tiled=True)  11.2 us
    ppermute x1, starting transfers between devices, shards(): own_panel = lax.ppermute(own_panel, ALL, TO_OWNER)  5.38 us
    all_to_all x1, starting transfers between devices, shards(): parts = lax.all_to_all(chip_sum, CHIPS_COL, 0, 0, tiled=True)  4.59 us
  transfers between devices with their start and end apart: 8, of which 6 were waited for; matrix products, arithmetic and copies ran while one was open for 2% of the time, Pallas kernels for 5%

profile of v2, /device:TPU:1, one launch (start us, length us, event | category | flops | bytes accessed | tf_op | source)
XLA Modules:
  0.0 174.2 jit_solution(2180816780966948442)
XLA Ops:
  0.6 1.2 copy-done
  1.9 1.4 fusion.1
  3.2 0.7 collective-permute-start
  3.9 0.3 broadcast_in_dim.36
  4.2 52.5 %all_to_all.20.mine_ref = f32[8,128,512]{2,1,0:T(8,128)S(1)} all-to-all(f32[8,128,512]{2,1,0:T(8,128)S(1)} %broadcast_in_dim.36), channel_id=1, replica_groups=mesh['z'=4,'yl'=2,'x'=4,'yh'=2,'c'=2] {'z','yl'}, dimensions={0} | all-to-all | bytes 4194304 | tf_op jit(solution)/shard_map/all_to_all | solution.py:52
  56.7 1.9 %collective-permute-start.1 = (f32[8,128,512]{2,1,0:T(8,128)S(1)}, f32[8,128,512]{2,1,0:T(8,128)}, u32[]{:S(2)}, u32[]{:S(2)}) collective-permute-start(f32[8,128,512]{2,1,0:T(8,128)S(1)} %all_to_all.20.mine_ref), channel_id=1, source_target_pairs={{0,1},{1,0},{2,3},{3,2},{4,5},{5,4},{6,7},{7,6},{8,9},{9,8},{10,11... | collective-permute-start | bytes 6291464 | tf_op jit(solution)/shard_map/ppermute | solution.py:118
  58.8 0.6 pad_add_fusion.1
  59.4 3.1 %collective-permute-done.1.other_ref = f32[8,128,512]{2,1,0:T(8,128)} collective-permute-done((f32[8,128,512]{2,1,0:T(8,128)S(1)}, f32[8,128,512]{2,1,0:T(8,128)}, u32[]{:S(2)}, u32[]{:S(2)}) %collective-permute-start.1) | collective-permute-done | bytes 2097184 | tf_op jit(solution)/shard_map/ppermute | solution.py:118
  62.5 9.0 %shard_map.69 = f32[8,128,512]{2,1,0:T(8,128)} custom-call(s32[9]{0:T(128)} %get-tuple-element.4.table, f32[8,2,128,1024]{3,2,1,0:T(8,128)} %bitcast.11, f32[8,128,512]{2,1,0:T(8,128)} %copy-done.1, f32[8,128,512]{2,1,0:T(8,128)} %collective-permute-done.1.other_ref), custom_call_target="tpu_custom_call" | custom-call | flops 3221225472 | bytes 10485760 | tf_op jit(solution)/shard_map/pallas_call | solution.py:84
  71.4 0.4 collective-permute-start.2
  71.8 8.9 %shard_map.68 = f32[8,128,512]{2,1,0:T(8,128)} custom-call(s32[9]{0:T(128)} %get-tuple-element.5.table, f32[8,2,128,1024]{3,2,1,0:T(8,128)} %bitcast.12, f32[8,128,512]{2,1,0:T(8,128)} %copy-done.1, f32[8,128,512]{2,1,0:T(8,128)} %collective-permute-done.1.other_ref), custom_call_target="tpu_custom_call" | custom-call | flops 3221225472 | bytes 10485760 | tf_op jit(solution)/shard_map/pallas_call | solution.py:84
  80.7 3.4 %add.60 = f32[8,128,512]{2,1,0:T(8,128)} add(f32[8,128,512]{2,1,0:T(8,128)} %shard_map.68, f32[8,128,512]{2,1,0:T(8,128)S(1)} %collective-permute-done.2) | non-fusion elementwise | flops 524288 | bytes 6291456 | tf_op jit(solution)/shard_map/add | solution.py:137
  84.1 4.6 %all-to-all-start.1 = ((f32[8,128,512]{2,1,0:T(8,128)}), f32[8,128,512]{2,1,0:T(8,128)S(1)}, u32[]{:S(2)}, u32[]{:S(2)}) async-start(f32[8,128,512]{2,1,0:T(8,128)} %add.60), calls=%async_computation.1 | async-start | bytes 4194304 | tf_op jit(solution)/shard_map/all_to_all | solution.py:138
  88.7 0.6 dynamic_slice.25
  90.6 1.8 %select_bitcast_fusion = f32[128,512]{1,0:T(8,128)} fusion(f32[8,128,512]{2,1,0:T(8,128)} %collective-permute-done.1.other_ref, s32[]{:T(128)S(6)} %select_n.54, f32[8,128,512]{2,1,0:T(8,128)} %copy-done.1, pred[]{:T(512)} %bitcast.3), kind=kLoop, calls=%fused_computation.2 | loop fusion | flops 65536 | bytes 786437 | tf_op jit(solution)/shard_map/jit(_where)/select_n | solution.py:126
  92.4 5.4 %collective-permute-start.3 = (f32[128,512]{1,0:T(8,128)}, f32[128,512]{1,0:T(8,128)}, u32[]{:S(2)}, u32[]{:S(2)}) collective-permute-start(f32[128,512]{1,0:T(8,128)} %select_bitcast_fusion), channel_id=1, source_target_pairs={{0,0},{1,8},{2,16},{3,24},{4,32},{5,40},{6,48},{7,56},{8,64},{9,72... | collective-permute-start | bytes 786440 | tf_op jit(solution)/shard_map/ppermute | solution.py:131
  97.7 22.3 %all-to-all-done.1 = f32[8,128,512]{2,1,0:T(8,128)S(1)} async-done(((f32[8,128,512]{2,1,0:T(8,128)}), f32[8,128,512]{2,1,0:T(8,128)S(1)}, u32[]{:S(2)}, u32[]{:S(2)}) %all-to-all-start.1) | async-done | bytes 2097184 | tf_op jit(solution)/shard_map/all_to_all | solution.py:138
  120.1 0.2 reduce_sum.28
  120.3 2.9 %collective-permute-done.3 = f32[128,512]{1,0:T(8,128)} collective-permute-done((f32[128,512]{1,0:T(8,128)}, f32[128,512]{1,0:T(8,128)}, u32[]{:S(2)}, u32[]{:S(2)}) %collective-permute-start.3) | collective-permute-done | bytes 262176 | tf_op jit(solution)/shard_map/ppermute | solution.py:131
  123.3 1.6 fusion.2
  125.0 1.9 %collective-permute-done.4 = f32[256,512]{1,0:T(8,128)S(1)} collective-permute-done((f32[256,512]{1,0:T(8,128)S(1)}, f32[256,512]{1,0:T(8,128)S(1)}, u32[]{:S(2)}, u32[]{:S(2)}) %collective-permute-start.4) | collective-permute-done | bytes 524320 | tf_op jit(solution)/shard_map/ppermute | solution.py:151
  127.0 0.9 reshape.23
  127.9 11.2 %all-to-all-start.2 = ((f32[64,4,512]{2,1,0:T(4,128)}), f32[64,4,512]{2,1,0:T(4,128)S(1)}, u32[]{:S(2)}, u32[]{:S(2)}) async-start(f32[64,4,512]{2,1,0:T(4,128)} %reshape.23), calls=%async_computation.2 | async-start | bytes 1048576 | tf_op jit(solution)/shard_map/all_to_all | solution.py:153
  139.1 12.4 %all-to-all-done.2 = f32[64,4,512]{2,1,0:T(4,128)S(1)} async-done(((f32[64,4,512]{2,1,0:T(4,128)}), f32[64,4,512]{2,1,0:T(4,128)S(1)}, u32[]{:S(2)}, u32[]{:S(2)}) %all-to-all-start.2) | async-done | bytes 524320 | tf_op jit(solution)/shard_map/all_to_all | solution.py:153
  151.5 0.1 reduce_sum.29
  151.6 0.7 dynamic-slice_subtract_fusion
  152.4 15.6 %all_to_all.21 = f32[64,4,512]{2,1,0:T(4,128)S(1)} all-to-all(f32[64,4,512]{2,1,0:T(4,128)S(1)} %broadcast_in_dim.38), channel_id=1, replica_groups=mesh['z'=4,'yl'=2,'x'=4,'yh'=2,'c'=2] {'z','yl','x','yh'}, dimensions={0} | all-to-all | bytes 1048576 | tf_op jit(solution)/shard_map/all_to_all | solution.py:52
  168.0 0.2 reshape.24
  168.2 3.3 %collective-permute-start.5 = (f32[256,512]{1,0:T(8,128)S(1)}, f32[256,512]{1,0:T(8,128)S(1)}, u32[]{:S(2)}, u32[]{:S(2)}) collective-permute-start(f32[256,512]{1,0:T(8,128)S(1)} %reshape.24), channel_id=1, source_target_pairs={{0,1},{1,0},{2,3},{3,2},{4,5},{5,4},{6,7},{7,6},{8,9},{9,8},{10,11... | collective-permute-start | bytes 1572872 | tf_op jit(solution)/shard_map/ppermute | solution.py:157
  171.5 1.5 collective-permute-done.5
  173.1 0.1 broadcast_select_fusion.1
  173.2 1.0 pad_maximum_fusion
  (16 shorter events, 0.5 us)
Async XLA Ops:
  0.6 1.2 copy-start
  3.2 0.7 collective-permute-start
  4.2 54.4 %copy-start.3 = (s32[128]{0:T(128)S(1)}, s32[128]{0:T(128)}, u32[]{:S(2)}) copy-start(s32[128]{0:T(128)} %param.9) | copy-start | bytes 1540
  56.7 5.8 %copy-start.1 = (f32[8,128,512]{2,1,0:T(8,128)}, f32[8,128,512]{2,1,0:T(8,128)S(1)}, u32[]{:S(2)}) copy-start(f32[8,128,512]{2,1,0:T(8,128)S(1)} %all_to_all.20.mine_ref) | copy-start | bytes 6291460
  56.7 5.8 %collective-permute-start.1 = (f32[8,128,512]{2,1,0:T(8,128)S(1)}, f32[8,128,512]{2,1,0:T(8,128)}, u32[]{:S(2)}, u32[]{:S(2)}) collective-permute-start(f32[8,128,512]{2,1,0:T(8,128)S(1)} %all_to_all.20.mine_ref), channel_id=1, source_target_pairs={{0,1},{1,0},{2,3},{3,2},{4,5},{5,4},{6,7},{7,6},{8,9},{9,8},{10,11... | collective-permute-start | bytes 6291464 | tf_op jit(solution)/shard_map/ppermute | solution.py:118
  71.4 9.3 %collective-permute-start.2 = (f32[8,128,512]{2,1,0:T(8,128)}, f32[8,128,512]{2,1,0:T(8,128)S(1)}, u32[]{:S(2)}, u32[]{:S(2)}) collective-permute-start(f32[8,128,512]{2,1,0:T(8,128)} %shard_map.69), channel_id=1, source_target_pairs={{0,1},{1,0},{2,3},{3,2},{4,5},{5,4},{6,7},{7,6},{8,9},{9,8},{10,11... | collective-permute-start | bytes 6291464 | tf_op jit(solution)/shard_map/ppermute | solution.py:137
  84.1 36.0 %all-to-all-start.1 = ((f32[8,128,512]{2,1,0:T(8,128)}), f32[8,128,512]{2,1,0:T(8,128)S(1)}, u32[]{:S(2)}, u32[]{:S(2)}) async-start(f32[8,128,512]{2,1,0:T(8,128)} %add.60), calls=%async_computation.1 | async-start | bytes 4194304 | tf_op jit(solution)/shard_map/all_to_all | solution.py:138
  92.4 30.9 %collective-permute-start.3 = (f32[128,512]{1,0:T(8,128)}, f32[128,512]{1,0:T(8,128)}, u32[]{:S(2)}, u32[]{:S(2)}) collective-permute-start(f32[128,512]{1,0:T(8,128)} %select_bitcast_fusion), channel_id=1, source_target_pairs={{0,0},{1,8},{2,16},{3,24},{4,32},{5,40},{6,48},{7,56},{8,64},{9,72... | collective-permute-start | bytes 786440 | tf_op jit(solution)/shard_map/ppermute | solution.py:131
  120.3 6.7 %copy-start.2 = (f32[128,512]{1,0:T(8,128)}, f32[128,512]{1,0:T(8,128)S(1)}, u32[]{:S(2)}) copy-start(f32[128,512]{1,0:T(8,128)S(1)} %neg.3) | copy-start | bytes 786436
  124.9 2.0 %collective-permute-start.4 = (f32[256,512]{1,0:T(8,128)S(1)}, f32[256,512]{1,0:T(8,128)S(1)}, u32[]{:S(2)}, u32[]{:S(2)}) collective-permute-start(f32[256,512]{1,0:T(8,128)S(1)} %constant_dynamic-slice_fusion), channel_id=1, source_target_pairs={{0,1},{1,0},{2,3},{3,2},{4,5},{5,4},{6,7},{7,6},{8,9},{9,8},{10,11... | collective-permute-start | bytes 1572872 | tf_op jit(solution)/shard_map/ppermute | solution.py:151
  127.9 23.6 %all-to-all-start.2 = ((f32[64,4,512]{2,1,0:T(4,128)}), f32[64,4,512]{2,1,0:T(4,128)S(1)}, u32[]{:S(2)}, u32[]{:S(2)}) async-start(f32[64,4,512]{2,1,0:T(4,128)} %reshape.23), calls=%async_computation.2 | async-start | bytes 1048576 | tf_op jit(solution)/shard_map/all_to_all | solution.py:153
  168.2 4.9 %collective-permute-start.5 = (f32[256,512]{1,0:T(8,128)S(1)}, f32[256,512]{1,0:T(8,128)S(1)}, u32[]{:S(2)}, u32[]{:S(2)}) collective-permute-start(f32[256,512]{1,0:T(8,128)S(1)} %reshape.24), channel_id=1, source_target_pairs={{0,1},{1,0},{2,3},{3,2},{4,5},{5,4},{6,7},{7,6},{8,9},{9,8},{10,11... | collective-permute-start | bytes 1572872 | tf_op jit(solution)/shard_map/ppermute | solution.py:157

commit v3 on v2

v3 whole, which is shorter than its diff:
```python
import jax
import jax.numpy as jnp
from jax import lax
from jax.experimental import pallas as pl
from jax.experimental.pallas import tpu as pltpu
from jax.sharding import Mesh, PartitionSpec as P

BLOCK = 128
ROW = ("z", "yl")
CHIPS_COL = ("x", "yh")
ALL = ("z", "yl", "x", "yh", "c")
CHIPS = ("z", "yl", "x", "yh")
HIGH = lax.Precision.HIGH
SWAP = [(0, 1), (1, 0)]
TILE = 2
VMEM_LIMIT = 24 * 1024 * 1024


def flat(z, yl, x, yh, c):
    return (z * 2 + yl) * 16 + x * 4 + yh * 2 + c


DEVICES = [
    (z, yl, x, yh, c)
    for z in range(4)
    for yl in range(2)
    for x in range(4)
    for yh in range(2)
    for c in range(2)
]
TO_COLUMN = [
    (flat(z, yl, x, yh, c), flat(x, yh ^ (x & 1), z, yl, c)) for z, yl, x, yh, c in DEVICES
]
TO_OWNER = [
    (flat(z, yl, x, yh, c), flat(x, yh, 2 * c + (z >> 1), yl ^ (z & 1), z & 1))
    for z, yl, x, yh, c in DEVICES
]


def dot(a, b):
    return jnp.dot(a, b, precision=HIGH, preferred_element_type=jnp.float32)


def spread(value, axes, count):
    copies = jnp.broadcast_to(value[None], (count,) + value.shape)
    return lax.all_to_all(copies, axes, 0, 0, tiled=True)


def split(value):
    high = value.astype(jnp.bfloat16)
    low = (value - high.astype(jnp.float32)).astype(jnp.bfloat16)
    return high, low


def whole_call(kernel, inputs, outputs, scratch=()):
    whole = pl.BlockSpec(memory_space=pltpu.VMEM)
    table, *arrays = inputs
    return pl.pallas_call(
        kernel,
        in_specs=[pl.BlockSpec(memory_space=pltpu.SMEM)] + [whole] * len(arrays),
        out_specs=[whole] * len(outputs),
        out_shape=outputs,
        scratch_shapes=scratch,
        compiler_params=pltpu.CompilerParams(vmem_limit_bytes=VMEM_LIMIT),
        cost_estimate=pl.CostEstimate(flops=4096, bytes_accessed=4096, transcendentals=0),
    )(table, *arrays)


def prepare_kernel(table, mine_ref, other_ref, high_ref, low_ref, own_ref):
    for s in range(16):
        source = mine_ref.at[s] if s < 8 else other_ref.at[s - 8]
        place = table[s]

        @pl.when((place >= 0) & (place < 8))
        def _():
            value = source[...]
            rows = pl.ds(pl.multiple_of(place * BLOCK, BLOCK), BLOCK)
            high, low = split(value)
            high_ref[rows, :] = high
            low_ref[rows, :] = low

            @pl.when(place == table[16])
            def _():
                own_ref[...] = value


def combine_kernel(table, keep_ref, taken_ref, out):
    out[...] = keep_ref[...] + taken_ref[...]


def total_kernel(table, parts, out, given, kept):
    value = parts[0]
    for k in range(1, 8):
        value = value + parts[k]
    value = -value
    half = value.shape[1] // 2
    out[...] = value
    first_core = table[17] == 0
    given[...] = jnp.where(first_core, value[:, half:], value[:, :half])
    kept[...] = jnp.where(first_core, value[:, :half], value[:, half:])


def assemble_kernel(table, mine, other, out):
    half = mine.shape[1]
    first_core = table[17] == 0
    out[:, :half] = jnp.where(first_core, mine[...], other[...])
    out[:, half:] = jnp.where(first_core, other[...], mine[...])


def half_kernel(table, a_ref, high_ref, low_ref, out_ref):
    rows = TILE * BLOCK
    a_high, a_low = split(a_ref[...].reshape(rows, a_ref.shape[-1]))
    total = jnp.dot(a_high, low_ref[...], preferred_element_type=jnp.float32)
    total += jnp.dot(a_low, high_ref[...], preferred_element_type=jnp.float32)
    total += jnp.dot(a_high, high_ref[...], preferred_element_type=jnp.float32)
    out_ref[...] = total.reshape(out_ref.shape)


def half_product(table, ancestor, high, low):
    depth, width = high.shape
    whole = pl.BlockSpec(memory_space=pltpu.VMEM)
    return pl.pallas_call(
        half_kernel,
        grid_spec=pltpu.PrefetchScalarGridSpec(
            num_scalar_prefetch=1,
            grid=(8 // TILE,),
            in_specs=[
                pl.BlockSpec((TILE, 1, BLOCK, depth), lambda i, table: (i, table[0], 0, 0)),
                whole,
                whole,
            ],
            out_specs=pl.BlockSpec((TILE, BLOCK, width), lambda i, table: (i, 0, 0)),
        ),
        out_shape=jax.ShapeDtypeStruct((8, BLOCK, width), jnp.float32),
        compiler_params=pltpu.CompilerParams(vmem_limit_bytes=VMEM_LIMIT),
        cost_estimate=pl.CostEstimate(
            flops=3 * 2 * 8 * BLOCK * depth * width,
            bytes_accessed=4 * (8 * BLOCK * depth + 2 * 8 * BLOCK * width),
            transcendentals=0,
        ),
    )(table, ancestor, high, low)


def shards(factor_panel, pivot_inverse, ancestor_inverse, diag_inverse, block_map):
    width = factor_panel.shape[1]
    core = lax.axis_index("c")
    z, yl = lax.axis_index("z"), lax.axis_index("yl")
    group = lax.axis_index(CHIPS_COL)

    half = width // 2
    first = lax.axis_index(CHIPS) * (width // 64)
    diag_piece = lax.dynamic_slice(diag_inverse, (first, core * half), (width // 64, half))
    half = width // 2
    first = lax.axis_index(CHIPS) * (width // 64)
    diag_piece = lax.dynamic_slice(diag_inverse, (first, core * half), (width // 64, half))
    row = jnp.arange(8, dtype=jnp.int32)
    columns = 2 * (row >> 1) + (row ^ (row >> 1)) % 2
    columns = jnp.concatenate([columns * 2 + core, columns * 2 + 1 - core])
    in_group = lax.dynamic_slice_in_dim(block_map, group * 16, 16) - group * 16
    chosen = columns[:, None] == jnp.arange(16, dtype=jnp.int32)[None, :]
    places = jnp.sum(jnp.where(chosen, in_group[None, :], 0), axis=1) - 8 * core
    send = (z >> 1) * 4 + (yl ^ (z & 1)) * 2 + (z & 1)
    places = jnp.concatenate([places, send[None], core[None]]).astype(jnp.int32)
    tables = [c[None].astype(jnp.int32) for c in (1 - core, core)]
    ancestor = ancestor_inverse.reshape(8, 2, BLOCK, ancestor_inverse.shape[1])
    ancestor = pltpu.with_memory_space_constraint(ancestor, pltpu.HBM)
    block = jax.ShapeDtypeStruct(factor_panel.shape, jnp.float32)
    blocks = jax.ShapeDtypeStruct((8,) + factor_panel.shape, jnp.float32)
    half_panel = jax.ShapeDtypeStruct((8 * BLOCK, width), jnp.bfloat16)

    moved = lax.ppermute(factor_panel, ALL, TO_COLUMN)
    column_block = dot(moved, pivot_inverse)
    column_block, places, tables, diag_piece = lax.optimization_barrier(
        (column_block, places, tables, diag_piece)
    )
    mine = spread(column_block, ROW, 8).reshape(8, BLOCK, width)
    other = lax.ppermute(mine, "c", SWAP)
    high, low, own = whole_call(
        prepare_kernel, [places, mine, other], [half_panel, half_panel, block]
    )
    own_panel = lax.ppermute(own, ALL, TO_OWNER)
    give = half_product(tables[0], ancestor, high, low)
    taken = lax.ppermute(give, "c", SWAP)
    keep = half_product(tables[1], ancestor, high, low)
    (chip_sum,) = whole_call(combine_kernel, [places, keep, taken], [blocks])
    chip_sum, own_panel = lax.optimization_barrier((chip_sum, own_panel))
    parts = lax.all_to_all(chip_sum, CHIPS_COL, 0, 0, tiled=True)
    columns = jax.ShapeDtypeStruct((BLOCK, half), jnp.float32)
    offdiag_block, given, kept = whole_call(
        total_kernel, [places, parts], [block, columns, columns]
    )

    def term(value):
        return lax.dot_general(
            own_panel,
            value,
            (((0,), (0,)), ((), ())),
            precision=HIGH,
            preferred_element_type=jnp.float32,
        )

    summed = lax.ppermute(term(given), "c", SWAP) + term(kept)
    summed, offdiag_block = lax.optimization_barrier((summed, offdiag_block))
    pieces = lax.all_to_all(summed.reshape(64, width // 64, half), CHIPS, 0, 0, tiled=True)
    mine_half = spread(diag_piece - jnp.sum(pieces, axis=0), CHIPS, 64).reshape(width, half)
    other_half = lax.ppermute(mine_half, "c", SWAP)
    (diag_block,) = whole_call(
        assemble_kernel,
        [places, mine_half, other_half],
        [jax.ShapeDtypeStruct(diag_inverse.shape, jnp.float32)],
    )
    return (offdiag_block, diag_block)


def solution(mesh):
    fine = Mesh(mesh.devices.reshape(4, 2, 4, 2, 2), ALL)
    rows, cols = ROW, ("x", "yh", "c")
    placed = (P(ALL, None), P(), P(rows, cols), P(), P())

    return jax.shard_map(
        shards,
        mesh=fine,
        in_specs=placed,
        out_specs=(P(ALL, None), P()),
        check_vma=False,
    )
```

time: 175 us -> 163 us (0.931)
  blocking collectives: 68.1 us -> 119 us
  waiting for transfers between devices: 44.2 us -> 15.1 us
  starting transfers between devices: 27.5 us -> 9.3 us
  other arithmetic: 8.29 us -> 1.24 us
  local copies, waits for them, and re-layouts: 3.31 us -> 0.31 us
  Pallas kernels: 17.8 us -> 16 us
    all_to_all x0 -> x2, blocking collectives: none -> 52.5 us  [the longest x1 33.7 us: shards(): parts = lax.all_to_all(chip_sum, CHIPS_COL, 0, 0, tiled=True)]
    all_to_all x2 -> x0, waiting for transfers between devices: 34.7 us -> none  [the longest x1 22.3 us: shards(): parts = lax.all_to_all(chip_sum, CHIPS_COL, 0, 0, tiled=True)]
    all_to_all x2 -> x0, starting transfers between devices: 15.8 us -> none  [the longest x1 11.2 us: shards(): lax.all_to_all(term.reshape(64, rows, width), CHIPS, 0, 0, tiled=True)]
    pallas_call x2, Pallas kernels: 17.8 us -> 11.3 us  [half_product(): pl.pallas_call(half_kernel, grid_spec=pltpu.PrefetchScalarGridSpec(num_sc...]
    ppermute x4, waiting for transfers between devices: 4.84 us -> 9.76 us  [the longest x1 8.27 us: shards(): own_panel = lax.ppermute(own, ALL, TO_OWNER)]
    pallas_call x0 -> x4, Pallas kernels: none -> 4.71 us  [whole_call(): pl.pallas_call(kernel, in_specs=[pl.BlockSpec(memory_space=pltpu.SMEM)] +...]
    add x3 -> x1, other arithmetic: 3.56 us -> 0.07 us  [shards(): summed = lax.ppermute(term(given), 'c', SWAP) + term(kept)]
    ppermute x4, starting transfers between devices: 6.52 us -> 4.17 us  [the longest x1 1.91 us: shards(): own_panel = lax.ppermute(own, ALL, TO_OWNER)]
  transfers between devices with their start and end apart: 8 -> 6, of which waited for: 6 -> 4; matrix products, arithmetic and copies ran while one was open for 2% -> 1% of each run, Pallas kernels for 5% -> 4%
where the time goes in v3:
time: 163 us
  blocking collectives  119 us (73%)
  Pallas kernels  16 us (10%)
  waiting for transfers between devices  15.1 us (9%)
  starting transfers between devices  9.3 us (6%)
    all_to_all x2, blocking collectives, spread(): return lax.all_to_all(copies, axes, 0, 0, tiled=True)  66.3 us
    all_to_all x1, blocking collectives, shards(): parts = lax.all_to_all(chip_sum, CHIPS_COL, 0, 0, tiled=True)  33.7 us
    all_to_all x1, blocking collectives, shards(): lax.all_to_all(summed.reshape(64, width // 64, half), CHIPS, 0, 0, tiled=...  18.8 us
    pallas_call x2, Pallas kernels, half_product(): pl.pallas_call(half_kernel, grid_spec=pltpu.PrefetchScalarGridSpec(num_sc...  11.3 us
    ppermute x1, waiting for transfers between devices, shards(): own_panel = lax.ppermute(own, ALL, TO_OWNER)  8.27 us
    pallas_call x4, Pallas kernels, whole_call(): pl.pallas_call(kernel, in_specs=[pl.BlockSpec(memory_space=pltpu.SMEM)] +...  4.71 us
    ppermute x1, waiting for transfers between devices, shards(): other = lax.ppermute(mine, 'c', SWAP)  3.79 us
  transfers between devices with their start and end apart: 6, of which 4 were waited for; matrix products, arithmetic and copies ran while one was open for 1% of the time, Pallas kernels for 4%

profile of v3, /device:TPU:1, one launch (start us, length us, event | category | flops | bytes accessed | tf_op | source)
XLA Modules:
  0.0 162.7 jit_solution(11131180873465896252)
XLA Ops:
  0.6 0.0 copy-start
  0.6 1.7 %collective-permute-start = (f32[128,512]{1,0:T(8,128)}, f32[128,512]{1,0:T(8,128)S(1)}, u32[]{:S(2)}, u32[]{:S(2)}) collective-permute-start(f32[128,512]{1,0:T(8,128)} %param.5), channel_id=1, source_target_pairs={{0,0},{1,1},{2,16},{3,17},{4,48},{5,49},{6,32},{7,33},{8,64},{9,65... | collective-permute-start | bytes 786440 | tf_op jit(solution)/shard_map/ppermute | solution.py:171
  2.4 0.7 dynamic-slice_subtract_fusion
  3.1 0.1 pad_add_fusion
  3.2 0.2 select_reduce_fusion
  3.4 0.1 pad_add_fusion.1.table
  3.5 0.4 fusion.4
  3.9 0.3 broadcast_in_dim.42
  4.2 50.7 %all_to_all.20.mine_ref = f32[8,128,512]{2,1,0:T(8,128)S(1)} all-to-all(f32[8,128,512]{2,1,0:T(8,128)S(1)} %broadcast_in_dim.42), channel_id=1, replica_groups=mesh['z'=4,'yl'=2,'x'=4,'yh'=2,'c'=2] {'z','yl'}, dimensions={0} | all-to-all | bytes 4194304 | tf_op jit(solution)/shard_map/all_to_all | solution.py:46
  54.9 1.9 %collective-permute-start.1 = (f32[8,128,512]{2,1,0:T(8,128)S(1)}, f32[8,128,512]{2,1,0:T(8,128)S(1)}, u32[]{:S(2)}, u32[]{:S(2)}) collective-permute-start(f32[8,128,512]{2,1,0:T(8,128)S(1)} %all_to_all.20.mine_ref), channel_id=1, source_target_pairs={{0,1},{1,0},{2,3},{3,2},{4,5},{5,4},{6,7},{7,6},{8,9},{9,8},{10,11... | collective-permute-start | bytes 6291464 | tf_op jit(solution)/shard_map/ppermute | solution.py:177
  56.7 3.8 %collective-permute-done.1.other_ref = f32[8,128,512]{2,1,0:T(8,128)S(1)} collective-permute-done((f32[8,128,512]{2,1,0:T(8,128)S(1)}, f32[8,128,512]{2,1,0:T(8,128)S(1)}, u32[]{:S(2)}, u32[]{:S(2)}) %collective-permute-start.1) | collective-permute-done | bytes 2097184 | tf_op jit(solution)/shard_map/ppermute | solution.py:177
  60.5 1.0 shard_map.68
  61.5 5.6 %shard_map.70 = f32[8,128,512]{2,1,0:T(8,128)S(1)} custom-call(s32[1]{0:T(128)} %bitcast.2.table, f32[8,2,128,1024]{3,2,1,0:T(8,128)} %bitcast.14, bf16[1024,512]{1,0:T(8,128)(2,1)S(1)} %get-tuple-element.20.high_ref, bf16[1024,512]{1,0:T(8,128)(2,1)S(1)} %get-tuple-element.21.low_ref), custom_call_target="tpu_custom_call" | custom-call | flops 3221225472 | bytes 8388608 | tf_op jit(solution)/shard_map/pallas_call | solution.py:122
  67.2 0.4 collective-permute-start.2
  67.6 1.9 %collective-permute-start.3 = (f32[128,512]{1,0:T(8,128)S(1)}, f32[128,512]{1,0:T(8,128)S(1)}, u32[]{:S(2)}, u32[]{:S(2)}) collective-permute-start(f32[128,512]{1,0:T(8,128)S(1)} %get-tuple-element.23), channel_id=1, source_target_pairs={{0,0},{1,8},{2,16},{3,24},{4,32},{5,40},{6,48},{7,56},{8,64},{9,72... | collective-permute-start | bytes 786440 | tf_op jit(solution)/shard_map/ppermute | solution.py:181
  69.5 5.6 %shard_map.69.keep_ref = f32[8,128,512]{2,1,0:T(8,128)S(1)} custom-call(s32[1]{0:T(128)} %bitcast.1.table, f32[8,2,128,1024]{3,2,1,0:T(8,128)} %bitcast.15, bf16[1024,512]{1,0:T(8,128)(2,1)S(1)} %get-tuple-element.20.high_ref, bf16[1024,512]{1,0:T(8,128)(2,1)S(1)} %get-tuple-element.21.low_ref), custom_call_target="tpu_custom_call" | custom-call | flops 3221225472 | bytes 8388608 | tf_op jit(solution)/shard_map/pallas_call | solution.py:122
  75.2 0.8 shard_map.71
  75.9 8.3 %collective-permute-done.3 = f32[128,512]{1,0:T(8,128)S(1)} collective-permute-done((f32[128,512]{1,0:T(8,128)S(1)}, f32[128,512]{1,0:T(8,128)S(1)}, u32[]{:S(2)}, u32[]{:S(2)}) %collective-permute-start.3) | collective-permute-done | bytes 262176 | tf_op jit(solution)/shard_map/ppermute | solution.py:181
  84.2 33.7 %all_to_all.21.parts = f32[8,128,512]{2,1,0:T(8,128)S(1)} all-to-all(f32[8,128,512]{2,1,0:T(8,128)S(1)} %shard_map.71), channel_id=1, replica_groups=mesh['z'=4,'yl'=2,'x'=4,'yh'=2,'c'=2] {'x','yh'}, dimensions={0} | all-to-all | bytes 4194304 | tf_op jit(solution)/shard_map/all_to_all | solution.py:187
  117.9 1.3 shard_map.72
  119.2 0.4 fusion.5
  119.6 0.0 dynamic-slice-start
  119.7 0.1 collective-permute-start.4
  119.8 0.4 fusion.6
  120.2 1.5 collective-permute-done.4
  121.7 0.1 add.63
  121.7 18.8 %all_to_all.22 = f32[64,8,256]{2,1,0:T(8,128)S(1)} all-to-all(f32[64,8,256]{2,1,0:T(8,128)S(1)} %bitcast.16), channel_id=1, replica_groups=mesh['z'=4,'yl'=2,'x'=4,'yh'=2,'c'=2] {'z','yl','x','yh'}, dimensions={0} | all-to-all | bytes 1048576 | tf_op jit(solution)/shard_map/all_to_all | solution.py:204
  140.6 0.1 reduce_sum.19
  140.7 15.6 %all_to_all.23 = f32[64,8,256]{2,1,0:T(8,128)S(1)} all-to-all(f32[64,8,256]{2,1,0:T(8,128)S(1)} %broadcast_in_dim.43), channel_id=1, replica_groups=mesh['z'=4,'yl'=2,'x'=4,'yh'=2,'c'=2] {'z','yl','x','yh'}, dimensions={0} | all-to-all | bytes 1048576 | tf_op jit(solution)/shard_map/all_to_all | solution.py:46
  156.3 3.3 %collective-permute-start.5 = (f32[512,256]{1,0:T(8,128)S(1)}, f32[512,256]{1,0:T(8,128)S(1)}, u32[]{:S(2)}, u32[]{:S(2)}) collective-permute-start(f32[512,256]{1,0:T(8,128)S(1)} %bitcast.12), channel_id=1, source_target_pairs={{0,1},{1,0},{2,3},{3,2},{4,5},{5,4},{6,7},{7,6},{8,9},{9,8},{10,11... | collective-permute-start | bytes 1572872 | tf_op jit(solution)/shard_map/ppermute | solution.py:206
  159.6 1.5 collective-permute-done.5.other
  161.1 1.6 shard_map.73
  (8 shorter events, 0.1 us)
Async XLA Ops:
  0.6 2.9 %copy-start = (f32[512,512]{1,0:T(8,128)S(1)}, f32[512,512]{1,0:T(8,128)}, u32[]{:S(2)}) copy-start(f32[512,512]{1,0:T(8,128)} %param.6) | copy-start | bytes 3145732
  0.6 2.8 %collective-permute-start = (f32[128,512]{1,0:T(8,128)}, f32[128,512]{1,0:T(8,128)S(1)}, u32[]{:S(2)}, u32[]{:S(2)}) collective-permute-start(f32[128,512]{1,0:T(8,128)} %param.5), channel_id=1, source_target_pairs={{0,0},{1,1},{2,16},{3,17},{4,48},{5,49},{6,32},{7,33},{8,64},{9,65... | collective-permute-start | bytes 786440 | tf_op jit(solution)/shard_map/ppermute | solution.py:171
  54.9 5.7 %collective-permute-start.1 = (f32[8,128,512]{2,1,0:T(8,128)S(1)}, f32[8,128,512]{2,1,0:T(8,128)S(1)}, u32[]{:S(2)}, u32[]{:S(2)}) collective-permute-start(f32[8,128,512]{2,1,0:T(8,128)S(1)} %all_to_all.20.mine_ref), channel_id=1, source_target_pairs={{0,1},{1,0},{2,3},{3,2},{4,5},{5,4},{6,7},{7,6},{8,9},{9,8},{10,11... | collective-permute-start | bytes 6291464 | tf_op jit(solution)/shard_map/ppermute | solution.py:177
  67.2 8.0 %collective-permute-start.2 = (f32[8,128,512]{2,1,0:T(8,128)S(1)}, f32[8,128,512]{2,1,0:T(8,128)S(1)}, u32[]{:S(2)}, u32[]{:S(2)}) collective-permute-start(f32[8,128,512]{2,1,0:T(8,128)S(1)} %shard_map.70), channel_id=1, source_target_pairs={{0,1},{1,0},{2,3},{3,2},{4,5},{5,4},{6,7},{7,6},{8,9},{9,8},{10,11... | collective-permute-start | bytes 6291464 | tf_op jit(solution)/shard_map/ppermute | solution.py:183
  67.6 16.6 %collective-permute-start.3 = (f32[128,512]{1,0:T(8,128)S(1)}, f32[128,512]{1,0:T(8,128)S(1)}, u32[]{:S(2)}, u32[]{:S(2)}) collective-permute-start(f32[128,512]{1,0:T(8,128)S(1)} %get-tuple-element.23), channel_id=1, source_target_pairs={{0,0},{1,8},{2,16},{3,24},{4,32},{5,40},{6,48},{7,56},{8,64},{9,72... | collective-permute-start | bytes 786440 | tf_op jit(solution)/shard_map/ppermute | solution.py:181
  119.6 21.0 %dynamic-slice-start = ((f32[512,512]{1,0:T(8,128)}, s32[]{:T(128)}, s32[]{:T(128)}), f32[8,256]{1,0:T(8,128)S(1)}, s32[]{:S(2)}) async-start(f32[512,512]{1,0:T(8,128)} %param.8, s32[]{:T(128)} %select_n.25, s32[]{:T(128)} %select_n.26), calls=%async_computation.4 | async-start | bytes 16896 | tf_op jit(solution)/shard_map/dynamic_slice | solution.py:155
  119.7 2.0 %collective-permute-start.4 = (f32[512,256]{1,0:T(8,128)S(1)}, f32[512,256]{1,0:T(8,128)S(1)}, u32[]{:S(2)}, u32[]{:S(2)}) collective-permute-start(f32[512,256]{1,0:T(8,128)S(1)} %fusion.5), channel_id=1, source_target_pairs={{0,1},{1,0},{2,3},{3,2},{4,5},{5,4},{6,7},{7,6},{8,9},{9,8},{10,11... | collective-permute-start | bytes 1572872 | tf_op jit(solution)/shard_map/ppermute | solution.py:202
  156.3 4.8 %collective-permute-start.5 = (f32[512,256]{1,0:T(8,128)S(1)}, f32[512,256]{1,0:T(8,128)S(1)}, u32[]{:S(2)}, u32[]{:S(2)}) collective-permute-start(f32[512,256]{1,0:T(8,128)S(1)} %bitcast.12), channel_id=1, source_target_pairs={{0,1},{1,0},{2,3},{3,2},{4,5},{5,4},{6,7},{7,6},{8,9},{9,8},{10,11... | collective-permute-start | bytes 1572872 | tf_op jit(solution)/shard_map/ppermute | solution.py:206

commit v4 on v3

v4 whole, which is shorter than its diff:
```python
import jax
import jax.numpy as jnp
from jax import lax
from jax.experimental import pallas as pl
from jax.experimental.pallas import tpu as pltpu
from jax.sharding import Mesh, PartitionSpec as P

BLOCK = 128
ROW = ("z", "yl")
CHIPS_COL = ("x", "yh")
ALL = ("z", "yl", "x", "yh", "c")
CHIPS = ("z", "yl", "x", "yh")
SWAP = [(0, 1), (1, 0)]
TILE = 2
VMEM_LIMIT = 24 * 1024 * 1024


def flat(z, yl, x, yh, c):
    return (z * 2 + yl) * 16 + x * 4 + yh * 2 + c


DEVICES = [
    (z, yl, x, yh, c)
    for z in range(4)
    for yl in range(2)
    for x in range(4)
    for yh in range(2)
    for c in range(2)
]
TO_COLUMN = [
    (flat(z, yl, x, yh, c), flat((z - x) % 4, yh ^ (x >> 1), z, yl, c))
    for z, yl, x, yh, c in DEVICES
]


def turn(k):
    return [(i, (i + k) % 4) for i in range(4)]


def split(value):
    high = value.astype(jnp.bfloat16)
    low = (value - high.astype(jnp.float32)).astype(jnp.bfloat16)
    return high, low


def whole_call(kernel, inputs, outputs, scratch=()):
    whole = pl.BlockSpec(memory_space=pltpu.VMEM)
    table, *arrays = inputs
    return pl.pallas_call(
        kernel,
        in_specs=[pl.BlockSpec(memory_space=pltpu.SMEM)] + [whole] * len(arrays),
        out_specs=[whole] * len(outputs),
        out_shape=outputs,
        scratch_shapes=scratch,
        compiler_params=pltpu.CompilerParams(vmem_limit_bytes=VMEM_LIMIT),
        cost_estimate=pl.CostEstimate(flops=4096, bytes_accessed=4096, transcendentals=0),
    )(table, *arrays)


def prepare_kernel(table, mine_ref, other_ref, high_ref, low_ref):
    for s in range(16):
        source = mine_ref.at[s] if s < 8 else other_ref.at[s - 8]
        place = table[s]

        @pl.when((place >= 0) & (place < 8))
        def _():
            rows = pl.ds(pl.multiple_of(place * BLOCK, BLOCK), BLOCK)
            high, low = split(source[...])
            high_ref[rows, :] = high
            low_ref[rows, :] = low


def order_kernel(table, mine_ref, other_ref, high_ref, low_ref):
    for s in range(16):
        source = mine_ref.at[s] if s < 8 else other_ref.at[s - 8]
        place = table[s]

        @pl.when((place & 1) == table[16])
        def _():
            lanes = pl.ds(pl.multiple_of((place >> 1) * BLOCK, BLOCK), BLOCK)
            high, low = split(source[...].T)
            high_ref[:, lanes] = high
            low_ref[:, lanes] = low


def product(left_high, left_low, value):
    high, low = split(value)
    total = jnp.dot(left_high, low, preferred_element_type=jnp.float32)
    total += jnp.dot(left_low, high, preferred_element_type=jnp.float32)
    total += jnp.dot(left_high, high, preferred_element_type=jnp.float32)
    return total


def given_kernel(table, high_ref, low_ref, value_ref, out):
    value = value_ref[...].reshape(8 * BLOCK, value_ref.shape[2])
    out[...] = product(high_ref[...], low_ref[...], value)


def kept_kernel(table, high_ref, low_ref, value_ref, taken_ref, out):
    value = value_ref[...].reshape(8 * BLOCK, value_ref.shape[2])
    total = product(high_ref[...], low_ref[...], value) + taken_ref[...]
    out[...] = total.reshape(out.shape)


def piece_kernel(table, base, pieces, out):
    value = base[...]
    for k in range(64):
        value = value + pieces[k]
    for k in range(64):
        out[k] = value


def norm_kernel(table, moved, pivot, out):
    out[...] = jnp.dot(
        moved[...],
        pivot[...],
        precision=lax.Precision.HIGHEST,
        preferred_element_type=jnp.float32,
    )


def spread_kernel(table, moved, pivot, out):
    value = jnp.dot(
        moved[...],
        pivot[...],
        precision=lax.Precision.HIGHEST,
        preferred_element_type=jnp.float32,
    )
    for k in range(8):
        out[k] = value


def pair_kernel(table, first, second, out):
    out[0] = first[...]
    out[1] = second[...]


def stack_kernel(table, *refs):
    for k in range(4):
        refs[4][2 * k : 2 * k + 2] = refs[k][...]


def combine_kernel(table, keep_ref, taken_ref, given, kept, *outs):
    half = given.shape[2]
    first_core = table[16] == 0
    for k in range(4):
        for y in range(2):
            i = ((table[17] + k) & 3) * 2 + y
            value = keep_ref[i] + taken_ref[i]
            outs[k][y] = value
            given[i] = jnp.where(first_core, value[:, half:], value[:, :half])
            kept[i] = jnp.where(first_core, value[:, :half], value[:, half:])


def line_kernel(table, own, first, second, third, keep, give):
    y = table[18]
    keep[...] = own[y] + first[y] + second[y] + third[y]
    give[...] = own[1 - y] + first[1 - y] + second[1 - y] + third[1 - y]


def total_kernel(table, keep, taken, out):
    out[...] = -(keep[...] + taken[...])


def assemble_kernel(table, mine, other, out):
    half = mine.shape[1]
    first_core = table[16] == 0
    out[:, :half] = jnp.where(first_core, mine[...], other[...])
    out[:, half:] = jnp.where(first_core, other[...], mine[...])


def half_kernel(table, a_ref, high_ref, low_ref, out_ref):
    rows = TILE * BLOCK

    @pl.loop(0, 8 // TILE)
    def _(i):
        tile = a_ref[pl.ds(i * TILE, TILE), table[0]]
        a_high, a_low = split(tile.reshape(rows, a_ref.shape[-1]))
        total = jnp.dot(a_high, low_ref[...], preferred_element_type=jnp.float32)
        total += jnp.dot(a_low, high_ref[...], preferred_element_type=jnp.float32)
        total += jnp.dot(a_high, high_ref[...], preferred_element_type=jnp.float32)
        out_ref[pl.ds(i * TILE, TILE)] = total.reshape(TILE, BLOCK, total.shape[-1])


def shards(factor_panel, pivot_inverse, ancestor_inverse, diag_inverse, block_map):
    width = factor_panel.shape[1]
    half = width // 2
    core = lax.axis_index("c")
    chip_row = lax.axis_index(ROW)
    group = lax.axis_index(CHIPS_COL)
    first = lax.axis_index(CHIPS) * (width // 64)
    diag_piece = lax.dynamic_slice(diag_inverse, (first, core * half), (width // 64, half))

    mine_at = jnp.stack([core, lax.axis_index("x"), lax.axis_index("yh")])

    def places(owner, chips, offset):
        columns = jnp.concatenate([chips * 2 + core, chips * 2 + 1 - core])
        in_group = lax.dynamic_slice_in_dim(block_map, owner * 16, 16) - owner * 16
        chosen = columns[:, None] == jnp.arange(16, dtype=jnp.int32)[None, :]
        found = jnp.sum(jnp.where(chosen, in_group[None, :], 0), axis=1) - offset
        return jnp.concatenate([found, mine_at]).astype(jnp.int32)

    row = jnp.arange(8, dtype=jnp.int32)
    x = (lax.axis_index("x") - (row >> 1)) & 3
    column_places = places(group, 2 * x + ((row ^ (x >> 1)) & 1), 8 * core)
    reach = (lax.axis_index("x") - (row >> 1)) & 3
    row_places = places(chip_row, 2 * reach + ((row & 1) ^ lax.axis_index("yh")), 0)
    tables = [c[None].astype(jnp.int32) for c in (1 - core, core)]
    ancestor = ancestor_inverse.reshape(8, 2, BLOCK, ancestor_inverse.shape[1])
    ancestor = pltpu.with_memory_space_constraint(ancestor, pltpu.VMEM)
    block = jax.ShapeDtypeStruct(factor_panel.shape, jnp.float32)
    blocks = jax.ShapeDtypeStruct((8,) + factor_panel.shape, jnp.float32)
    half_blocks = jax.ShapeDtypeStruct((8, BLOCK, half), jnp.float32)
    half_panel = jax.ShapeDtypeStruct((8 * BLOCK, width), jnp.bfloat16)

    moved = lax.ppermute(factor_panel, ALL, TO_COLUMN)
    panel, pivot_inverse, column_places, row_places, tables, diag_piece = (
        lax.optimization_barrier(
            (factor_panel, pivot_inverse, column_places, row_places, tables, diag_piece)
        )
    )
    pair = jax.ShapeDtypeStruct((2, BLOCK, width), jnp.float32)
    (normed,) = whole_call(norm_kernel, [row_places, panel, pivot_inverse], [block])
    beside = lax.ppermute(normed, "yh", SWAP)
    row_lines = list(whole_call(pair_kernel, [row_places, normed, beside], [pair]))
    for k in range(1, 4):
        row_lines.append(lax.ppermute(row_lines[0], "x", turn(k)))
    moved, ancestor = lax.optimization_barrier((moved, ancestor))
    (copies,) = whole_call(spread_kernel, [column_places, moved, pivot_inverse], [blocks])
    mine = lax.all_to_all(copies, ROW, 0, 0, tiled=True)
    other = lax.ppermute(mine, "c", SWAP)
    high, low = whole_call(prepare_kernel, [column_places, mine, other], [half_panel, half_panel])
    (row_mine,) = whole_call(stack_kernel, [row_places, *row_lines], [blocks])
    row_other = lax.ppermute(row_mine, "c", SWAP)
    turned = jax.ShapeDtypeStruct((width, 8 * BLOCK), jnp.bfloat16)
    row_high, row_low = whole_call(
        order_kernel, [row_places, row_mine, row_other], [turned, turned]
    )
    (give,) = whole_call(half_kernel, [tables[0], ancestor, high, low], [blocks])
    taken = lax.ppermute(give, "c", SWAP)
    (keep,) = whole_call(half_kernel, [tables[1], ancestor, high, low], [blocks])
    given, kept, *lines = whole_call(
        combine_kernel, [row_places, keep, taken], [half_blocks, half_blocks] + [pair] * 4
    )
    (given,) = whole_call(
        given_kernel,
        [row_places, row_high, row_low, given],
        [jax.ShapeDtypeStruct((width, half), jnp.float32)],
    )
    given = lax.ppermute(given, "c", SWAP)
    for k in range(1, 4):
        lines[k] = lax.ppermute(lines[k], "x", turn(k))
    slabs = jax.ShapeDtypeStruct((64, width // 64, half), jnp.float32)
    (summed,) = whole_call(
        kept_kernel, [row_places, row_high, row_low, kept, given], [slabs]
    )
    pieces = lax.all_to_all(summed, CHIPS, 0, 0, tiled=True)
    (copies,) = whole_call(piece_kernel, [row_places, diag_piece, pieces], [slabs])
    keep_line, give_line = whole_call(line_kernel, [row_places, *lines], [block, block])
    take_line = lax.ppermute(give_line, "yh", SWAP)
    mine_half = lax.all_to_all(copies, CHIPS, 0, 0, tiled=True).reshape(width, half)
    other_half = lax.ppermute(mine_half, "c", SWAP)
    (offdiag_block,) = whole_call(total_kernel, [row_places, keep_line, take_line], [block])
    (diag_block,) = whole_call(
        assemble_kernel,
        [row_places, mine_half, other_half],
        [jax.ShapeDtypeStruct(diag_inverse.shape, jnp.float32)],
    )
    return (offdiag_block, diag_block)


def solution(mesh):
    fine = Mesh(mesh.devices.reshape(4, 2, 4, 2, 2), ALL)
    rows, cols = ROW, ("x", "yh", "c")
    placed = (P(ALL, None), P(), P(rows, cols), P(), P())

    return jax.shard_map(
        shards,
        mesh=fine,
        in_specs=placed,
        out_specs=(P(ALL, None), P()),
        check_vma=False,
    )
```

time: 163 us -> 185 us (1.13); the launches traced: 163 us -> 182 us
  blocking collectives: 119 us -> 68.9 us
  waiting for transfers between devices: 15.1 us -> 55.1 us
  starting transfers between devices: 9.3 us -> 29.3 us
  Pallas kernels: 16 us -> 24.4 us
    all_to_all x4 -> x2, blocking collectives: 119 us -> 68.9 us  [the longest x1 50.4 us: shards(): mine = lax.all_to_all(copies, ROW, 0, 0, tiled=True)]
    ppermute x2 -> x10, waiting for transfers between devices: 9.75 us -> 48.9 us  [the longest x3 22.4 us: shards(): row_lines.append(lax.ppermute(row_lines[0], 'x', turn(k)))]
    pallas_call x4 -> x15, Pallas kernels: 4.71 us -> 24.4 us  [whole_call(): pl.pallas_call(kernel, in_specs=[pl.BlockSpec(memory_space=pltpu.SMEM)] +...]
    ppermute x2 -> x10, starting transfers between devices: 1.99 us -> 15.1 us  [the longest x3 4.66 us: shards(): lines[k] = lax.ppermute(lines[k], 'x', turn(k))]
    pallas_call x2 -> x0, Pallas kernels: 11.3 us -> none  [half_product(): pl.pallas_call(half_kernel, grid_spec=pltpu.PrefetchScalarGridSpec(num_sc...]
    all_to_all x0 -> x1, waiting for transfers between devices: none -> 6.22 us  [shards(): lax.all_to_all(copies, CHIPS, 0, 0, tiled=True).reshape(width, half)]
    all_to_all x0 -> x1, starting transfers between devices: none -> 4.77 us  [shards(): lax.all_to_all(copies, CHIPS, 0, 0, tiled=True).reshape(width, half)]
    ppermute x1, waiting for transfers between devices: 3.79 us -> 0.01 us  [shards(): other = lax.ppermute(mine, 'c', SWAP)]
  transfers between devices with their start and end apart: 6 -> 15, of which waited for: 4 -> 8; matrix products, arithmetic and copies ran while one was open for 1% -> 1% of each run, Pallas kernels for 4% -> 8%
where the time goes in v4:
time: 185 us; the launch traced here: 182 us
  blocking collectives  68.9 us (37%)
  waiting for transfers between devices  55.1 us (30%)
  starting transfers between devices  29.3 us (16%)
  Pallas kernels  24.4 us (13%)
  local copies, waits for them, and re-layouts  1.95 us (1%)
    all_to_all x1, blocking collectives, shards(): mine = lax.all_to_all(copies, ROW, 0, 0, tiled=True)  50.4 us
    pallas_call x15, Pallas kernels, whole_call(): pl.pallas_call(kernel, in_specs=[pl.BlockSpec(memory_space=pltpu.SMEM)] +...  24.4 us
    ppermute x3, waiting for transfers between devices, shards(): row_lines.append(lax.ppermute(row_lines[0], 'x', turn(k)))  22.4 us
    all_to_all x1, blocking collectives, shards(): pieces = lax.all_to_all(summed, CHIPS, 0, 0, tiled=True)  18.5 us
    ppermute x3, waiting for transfers between devices, shards(): lines[k] = lax.ppermute(lines[k], 'x', turn(k))  12.4 us
    ppermute x1, waiting for transfers between devices, shards(): beside = lax.ppermute(normed, 'yh', SWAP)  8.58 us
    all_to_all x1, waiting for transfers between devices, shards(): lax.all_to_all(copies, CHIPS, 0, 0, tiled=True).reshape(width, half)  6.22 us
    ppermute x1, starting transfers between devices, shards(): other_half = lax.ppermute(mine_half, 'c', SWAP)  5.85 us
  transfers between devices with their start and end apart: 15, of which 8 were waited for; matrix products, arithmetic and copies ran while one was open for 1% of the time, Pallas kernels for 8%

profile of v4, /device:TPU:1, one launch (start us, length us, event | category | flops | bytes accessed | tf_op | source)
XLA Modules:
  0.0 182.0 jit_solution(3497964717986224127)
XLA Ops:
  0.6 1.6 collective-permute-start
  4.5 1.2 copy-done
  5.7 1.3 shard_map.68
  7.0 50.4 %all_to_all.15.mine_ref = f32[8,128,512]{2,1,0:T(8,128)S(1)} all-to-all(f32[8,128,512]{2,1,0:T(8,128)S(1)} %shard_map.68), channel_id=1, replica_groups=mesh['z'=4,'yl'=2,'x'=4,'yh'=2,'c'=2] {'z','yl'}, dimensions={0} | all-to-all | bytes 4194304 | tf_op jit(solution)/shard_map/all_to_all | solution.py:230
  57.4 1.8 %collective-permute-start.1 = (f32[8,128,512]{2,1,0:T(8,128)S(1)}, f32[8,128,512]{2,1,0:T(8,128)S(1)}, u32[]{:S(2)}, u32[]{:S(2)}) collective-permute-start(f32[8,128,512]{2,1,0:T(8,128)S(1)} %all_to_all.15.mine_ref), channel_id=1, source_target_pairs={{0,1},{1,0},{2,3},{3,2},{4,5},{5,4},{6,7},{7,6},{8,9},{9,8},{10,11... | collective-permute-start | bytes 6291464 | tf_op jit(solution)/shard_map/ppermute | solution.py:231
  59.3 1.2 shard_map.75.first
  61.4 8.6 %collective-permute-done.7.second = f32[128,512]{1,0:T(8,128)S(1)} collective-permute-done((f32[128,512]{1,0:T(8,128)S(1)}, f32[128,512]{1,0:T(8,128)S(1)}, u32[]{:S(2)}, u32[]{:S(2)}) %collective-permute-start.7) | collective-permute-done | bytes 262176 | tf_op jit(solution)/shard_map/ppermute | solution.py:224
  70.9 4.1 %collective-permute-start.9 = (f32[2,128,512]{2,1,0:T(8,128)S(1)}, f32[2,128,512]{2,1,0:T(8,128)S(1)}, u32[]{:S(2)}, u32[]{:S(2)}) collective-permute-start(f32[2,128,512]{2,1,0:T(8,128)S(1)} %shard_map.76.refs_0_), channel_id=1, source_target_pairs={{0,8},{4,12},{8,0},{12,4},{1,9},{5,13},{9,1},{13,5},{2,10},{6,14},... | collective-permute-start | bytes 1572872 | tf_op jit(solution)/shard_map/ppermute | solution.py:227
  75.0 10.2 %collective-permute-done.8.refs_1_ = f32[2,128,512]{2,1,0:T(8,128)S(1)} collective-permute-done((f32[2,128,512]{2,1,0:T(8,128)S(1)}, f32[2,128,512]{2,1,0:T(8,128)S(1)}, u32[]{:S(2)}, u32[]{:S(2)}) %collective-permute-start.8) | collective-permute-done | bytes 524320 | tf_op jit(solution)/shard_map/ppermute | solution.py:227
  85.2 12.1 %collective-permute-done.9.refs_2_ = f32[2,128,512]{2,1,0:T(8,128)S(1)} collective-permute-done((f32[2,128,512]{2,1,0:T(8,128)S(1)}, f32[2,128,512]{2,1,0:T(8,128)S(1)}, u32[]{:S(2)}, u32[]{:S(2)}) %collective-permute-start.9) | collective-permute-done | bytes 524320 | tf_op jit(solution)/shard_map/ppermute | solution.py:227
  98.1 1.8 collective-permute-start.11
  100.9 4.0 %shard_map.71 = f32[8,128,512]{2,1,0:T(8,128)S(1)} custom-call(s32[1]{0:T(128)} %bitcast.3.table, f32[8,2,128,1024]{3,2,1,0:T(8,128)S(1)} %bitcast.8, bf16[1024,512]{1,0:T(8,128)(2,1)S(1)} %get-tuple-element.29.high_ref, bf16[1024,512]{1,0:T(8,128)(2,1)S(1)} %get-tuple-element.30.low_ref), custom_call_target="tpu_custom_call" | custom-call | flops 4096 | bytes 4096 | tf_op jit(solution)/shard_map/pallas_call | solution.py:49
  105.0 1.8 %shard_map.78 = (bf16[512,1024]{1,0:T(8,128)(2,1)S(1)}, bf16[512,1024]{1,0:T(8,128)(2,1)S(1)}) custom-call(s32[19]{0:T(128)S(1)} %add_add_fusion.1.table, f32[8,128,512]{2,1,0:T(8,128)S(1)} %shard_map.77.mine_ref, f32[8,128,512]{2,1,0:T(8,128)S(1)} %collective-permute-done.11.other_ref), custom_call_target="tpu_custom_call" | custom-call | flops 4096 | bytes 4096 | tf_op jit(solution)/shard_map/pallas_call | solution.py:49
  106.8 4.0 %shard_map.70.keep_ref = f32[8,128,512]{2,1,0:T(8,128)S(1)} custom-call(s32[1]{0:T(128)} %bitcast.table, f32[8,2,128,1024]{3,2,1,0:T(8,128)S(1)} %bitcast.9, bf16[1024,512]{1,0:T(8,128)(2,1)S(1)} %get-tuple-element.29.high_ref, bf16[1024,512]{1,0:T(8,128)(2,1)S(1)} %get-tuple-element.30.low_ref), custom_call_target="tpu_custom_call" | custom-call | flops 4096 | bytes 4096 | tf_op jit(solution)/shard_map/pallas_call | solution.py:49
  110.8 1.8 shard_map.72
  112.6 1.5 shard_map.79
  114.7 1.5 collective-permute-done.12.taken_ref
  116.3 1.5 shard_map.80
  117.8 18.5 %all_to_all.16.pieces = f32[64,8,256]{2,1,0:T(8,128)S(1)} all-to-all(f32[64,8,256]{2,1,0:T(8,128)S(1)} %shard_map.80), channel_id=1, replica_groups=mesh['z'=4,'yl'=2,'x'=4,'yh'=2,'c'=2] {'z','yl','x','yh'}, dimensions={0} | all-to-all | bytes 1048576 | tf_op jit(solution)/shard_map/all_to_all | solution.py:257
  136.3 1.5 shard_map.81
  137.8 4.8 %all-to-all-start.2 = ((f32[64,8,256]{2,1,0:T(8,128)}), f32[64,8,256]{2,1,0:T(8,128)S(1)}, u32[]{:S(2)}, u32[]{:S(2)}) async-start(f32[64,8,256]{2,1,0:T(8,128)} %shard_map.81), calls=%async_computation.2 | async-start | bytes 1048576 | tf_op jit(solution)/shard_map/all_to_all | solution.py:261
  142.6 1.1 collective-permute-start.3
  143.6 2.4 %collective-permute-start.4 = (f32[2,128,512]{2,1,0:T(8,128)}, f32[2,128,512]{2,1,0:T(8,128)S(1)}, u32[]{:S(2)}, u32[]{:S(2)}) collective-permute-start(f32[2,128,512]{2,1,0:T(8,128)} %get-tuple-element.34), channel_id=1, source_target_pairs={{0,8},{4,12},{8,0},{12,4},{1,9},{5,13},{9,1},{13,5},{2,10},{6,14},... | collective-permute-start | bytes 1572872 | tf_op jit(solution)/shard_map/ppermute | solution.py:252
  146.0 1.2 collective-permute-start.5
  147.2 6.2 %all-to-all-done.2 = f32[64,8,256]{2,1,0:T(8,128)S(1)} async-done(((f32[64,8,256]{2,1,0:T(8,128)}), f32[64,8,256]{2,1,0:T(8,128)S(1)}, u32[]{:S(2)}, u32[]{:S(2)}) %all-to-all-start.2) | async-done | bytes 524320 | tf_op jit(solution)/shard_map/all_to_all | solution.py:261
  153.4 5.9 %collective-permute-start.13 = (f32[512,256]{1,0:T(8,128)S(1)}, f32[512,256]{1,0:T(8,128)S(1)}, u32[]{:S(2)}, u32[]{:S(2)}) collective-permute-start(f32[512,256]{1,0:T(8,128)S(1)} %bitcast.10), channel_id=1, source_target_pairs={{0,1},{1,0},{2,3},{3,2},{4,5},{5,4},{6,7},{7,6},{8,9},{9,8},{10,11... | collective-permute-start | bytes 1572872 | tf_op jit(solution)/shard_map/ppermute | solution.py:262
  159.3 3.0 %collective-permute-done.3.first = f32[2,128,512]{2,1,0:T(8,128)S(1)} collective-permute-done((f32[2,128,512]{2,1,0:T(8,128)}, f32[2,128,512]{2,1,0:T(8,128)S(1)}, u32[]{:S(2)}, u32[]{:S(2)}) %collective-permute-start.3) | collective-permute-done | bytes 524320 | tf_op jit(solution)/shard_map/ppermute | solution.py:252
  162.3 9.4 %collective-permute-done.4.second = f32[2,128,512]{2,1,0:T(8,128)S(1)} collective-permute-done((f32[2,128,512]{2,1,0:T(8,128)}, f32[2,128,512]{2,1,0:T(8,128)S(1)}, u32[]{:S(2)}, u32[]{:S(2)}) %collective-permute-start.4) | collective-permute-done | bytes 524320 | tf_op jit(solution)/shard_map/ppermute | solution.py:252
  172.3 2.8 %collective-permute-start.6 = (f32[128,512]{1,0:T(8,128)S(1)}, f32[128,512]{1,0:T(8,128)S(1)}, u32[]{:S(2)}, u32[]{:S(2)}) collective-permute-start(f32[128,512]{1,0:T(8,128)S(1)} %get-tuple-element.37), channel_id=1, source_target_pairs={{0,2},{2,0},{1,3},{3,1},{4,6},{6,4},{5,7},{7,5},{8,10},{10,8},{9,1... | collective-permute-start | bytes 786440 | tf_op jit(solution)/shard_map/ppermute | solution.py:260
  175.1 4.0 %collective-permute-done.6.taken = f32[128,512]{1,0:T(8,128)S(1)} collective-permute-done((f32[128,512]{1,0:T(8,128)S(1)}, f32[128,512]{1,0:T(8,128)S(1)}, u32[]{:S(2)}, u32[]{:S(2)}) %collective-permute-start.6) | collective-permute-done | bytes 262176 | tf_op jit(solution)/shard_map/ppermute | solution.py:260
  179.1 1.3 shard_map.74
  180.4 1.6 shard_map.82
  (37 shorter events, 6.9 us)
Async XLA Ops:
  0.6 3.8 %collective-permute-start = (f32[128,512]{1,0:T(8,128)}, f32[128,512]{1,0:T(8,128)S(1)}, u32[]{:S(2)}, u32[]{:S(2)}) collective-permute-start(f32[128,512]{1,0:T(8,128)} %moved), channel_id=1, source_target_pairs={{0,0},{1,1},{2,16},{3,17},{4,96},{5,97},{6,112},{7,113},{8,80},{9,... | collective-permute-start | bytes 786440 | tf_op jit(solution)/shard_map/ppermute | solution.py:216
  4.5 1.2 copy-start
  5.7 53.6 %copy-start.1 = (f32[512,512]{1,0:T(8,128)S(1)}, f32[512,512]{1,0:T(8,128)}, u32[]{:S(2)}) copy-start(f32[512,512]{1,0:T(8,128)} %pivot.1) | copy-start | bytes 3145732
  5.7 53.6 %copy-start.2 = (f32[128,512]{1,0:T(8,128)S(1)}, f32[128,512]{1,0:T(8,128)}, u32[]{:S(2)}) copy-start(f32[128,512]{1,0:T(8,128)} %moved) | copy-start | bytes 786436
  7.0 93.9 %slice-start = ((s8[8388608]{0:T(1024)(128)(4,1)}), s8[4194304]{0:T(1024)(128)(4,1)S(1)}, s32[]{:S(2)}) async-start(s8[8388608]{0:T(1024)(128)(4,1)} %bitcast.6), calls=%async_computation.3 | async-start | bytes 8388608
  57.4 42.4 %collective-permute-start.1 = (f32[8,128,512]{2,1,0:T(8,128)S(1)}, f32[8,128,512]{2,1,0:T(8,128)S(1)}, u32[]{:S(2)}, u32[]{:S(2)}) collective-permute-start(f32[8,128,512]{2,1,0:T(8,128)S(1)} %all_to_all.15.mine_ref), channel_id=1, source_target_pairs={{0,1},{1,0},{2,3},{3,2},{4,5},{5,4},{6,7},{7,6},{8,9},{9,8},{10,11... | collective-permute-start | bytes 6291464 | tf_op jit(solution)/shard_map/ppermute | solution.py:231
  60.5 9.4 %collective-permute-start.7 = (f32[128,512]{1,0:T(8,128)S(1)}, f32[128,512]{1,0:T(8,128)S(1)}, u32[]{:S(2)}, u32[]{:S(2)}) collective-permute-start(f32[128,512]{1,0:T(8,128)S(1)} %shard_map.75.first), channel_id=1, source_target_pairs={{0,2},{2,0},{1,3},{3,1},{4,6},{6,4},{5,7},{7,5},{8,10},{10,8},{9,1... | collective-permute-start | bytes 786440 | tf_op jit(solution)/shard_map/ppermute | solution.py:224
  70.5 30.3 %slice-start.1 = ((s8[8388608]{0:T(1024)(128)(4,1)}), s8[4194304]{0:T(1024)(128)(4,1)S(1)}, s32[]{:S(2)}) async-start(s8[8388608]{0:T(1024)(128)(4,1)} %bitcast.6), calls=%async_computation.4 | async-start | bytes 8388608
  70.5 14.7 %collective-permute-start.8 = (f32[2,128,512]{2,1,0:T(8,128)S(1)}, f32[2,128,512]{2,1,0:T(8,128)S(1)}, u32[]{:S(2)}, u32[]{:S(2)}) collective-permute-start(f32[2,128,512]{2,1,0:T(8,128)S(1)} %shard_map.76.refs_0_), channel_id=1, source_target_pairs={{0,4},{4,8},{8,12},{12,0},{1,5},{5,9},{9,13},{13,1},{2,6},{6,10},{... | collective-permute-start | bytes 1572872 | tf_op jit(solution)/shard_map/ppermute | solution.py:227
  70.9 26.5 %collective-permute-start.9 = (f32[2,128,512]{2,1,0:T(8,128)S(1)}, f32[2,128,512]{2,1,0:T(8,128)S(1)}, u32[]{:S(2)}, u32[]{:S(2)}) collective-permute-start(f32[2,128,512]{2,1,0:T(8,128)S(1)} %shard_map.76.refs_0_), channel_id=1, source_target_pairs={{0,8},{4,12},{8,0},{12,4},{1,9},{5,13},{9,1},{13,5},{2,10},{6,14},... | collective-permute-start | bytes 1572872 | tf_op jit(solution)/shard_map/ppermute | solution.py:227
  75.0 22.4 %collective-permute-start.10 = (f32[2,128,512]{2,1,0:T(8,128)S(1)}, f32[2,128,512]{2,1,0:T(8,128)S(1)}, u32[]{:S(2)}, u32[]{:S(2)}) collective-permute-start(f32[2,128,512]{2,1,0:T(8,128)S(1)} %shard_map.76.refs_0_), channel_id=1, source_target_pairs={{0,12},{4,0},{8,4},{12,8},{1,13},{5,1},{9,5},{13,9},{2,14},{6,2},{... | collective-permute-start | bytes 1572872 | tf_op jit(solution)/shard_map/ppermute | solution.py:227
  98.1 6.9 %collective-permute-start.11 = (f32[8,128,512]{2,1,0:T(8,128)S(1)}, f32[8,128,512]{2,1,0:T(8,128)S(1)}, u32[]{:S(2)}, u32[]{:S(2)}) collective-permute-start(f32[8,128,512]{2,1,0:T(8,128)S(1)} %shard_map.77.mine_ref), channel_id=1, source_target_pairs={{0,1},{1,0},{2,3},{3,2},{4,5},{5,4},{6,7},{7,6},{8,9},{9,8},{10,11... | collective-permute-start | bytes 6291464 | tf_op jit(solution)/shard_map/ppermute | solution.py:234
  104.9 5.9 %collective-permute-start.2 = (f32[8,128,512]{2,1,0:T(8,128)S(1)}, f32[8,128,512]{2,1,0:T(8,128)S(1)}, u32[]{:S(2)}, u32[]{:S(2)}) collective-permute-start(f32[8,128,512]{2,1,0:T(8,128)S(1)} %shard_map.71), channel_id=1, source_target_pairs={{0,1},{1,0},{2,3},{3,2},{4,5},{5,4},{6,7},{7,6},{8,9},{9,8},{10,11... | collective-permute-start | bytes 6291464 | tf_op jit(solution)/shard_map/ppermute | solution.py:240
  114.1 2.1 %collective-permute-start.12 = (f32[512,256]{1,0:T(8,128)S(1)}, f32[512,256]{1,0:T(8,128)S(1)}, u32[]{:S(2)}, u32[]{:S(2)}) collective-permute-start(f32[512,256]{1,0:T(8,128)S(1)} %shard_map.79), channel_id=1, source_target_pairs={{0,1},{1,0},{2,3},{3,2},{4,5},{5,4},{6,7},{7,6},{8,9},{9,8},{10,11... | collective-permute-start | bytes 1572872 | tf_op jit(solution)/shard_map/ppermute | solution.py:250
  137.8 15.7 %all-to-all-start.2 = ((f32[64,8,256]{2,1,0:T(8,128)}), f32[64,8,256]{2,1,0:T(8,128)S(1)}, u32[]{:S(2)}, u32[]{:S(2)}) async-start(f32[64,8,256]{2,1,0:T(8,128)} %shard_map.81), calls=%async_computation.2 | async-start | bytes 1048576 | tf_op jit(solution)/shard_map/all_to_all | solution.py:261
  142.6 19.7 %collective-permute-start.3 = (f32[2,128,512]{2,1,0:T(8,128)}, f32[2,128,512]{2,1,0:T(8,128)S(1)}, u32[]{:S(2)}, u32[]{:S(2)}) collective-permute-start(f32[2,128,512]{2,1,0:T(8,128)} %get-tuple-element.33), channel_id=1, source_target_pairs={{0,4},{4,8},{8,12},{12,0},{1,5},{5,9},{9,13},{13,1},{2,6},{6,10},{... | collective-permute-start | bytes 1572872 | tf_op jit(solution)/shard_map/ppermute | solution.py:252
  143.6 28.0 %collective-permute-start.4 = (f32[2,128,512]{2,1,0:T(8,128)}, f32[2,128,512]{2,1,0:T(8,128)S(1)}, u32[]{:S(2)}, u32[]{:S(2)}) collective-permute-start(f32[2,128,512]{2,1,0:T(8,128)} %get-tuple-element.34), channel_id=1, source_target_pairs={{0,8},{4,12},{8,0},{12,4},{1,9},{5,13},{9,1},{13,5},{2,10},{6,14},... | collective-permute-start | bytes 1572872 | tf_op jit(solution)/shard_map/ppermute | solution.py:252
  146.0 25.6 %collective-permute-start.5 = (f32[2,128,512]{2,1,0:T(8,128)S(1)}, f32[2,128,512]{2,1,0:T(8,128)S(1)}, u32[]{:S(2)}, u32[]{:S(2)}) collective-permute-start(f32[2,128,512]{2,1,0:T(8,128)S(1)} %get-tuple-element.35), channel_id=1, source_target_pairs={{0,12},{4,0},{8,4},{12,8},{1,13},{5,1},{9,5},{13,9},{2,14},{6,2},{... | collective-permute-start | bytes 1572872 | tf_op jit(solution)/shard_map/ppermute | solution.py:252
  153.4 26.9 %collective-permute-start.13 = (f32[512,256]{1,0:T(8,128)S(1)}, f32[512,256]{1,0:T(8,128)S(1)}, u32[]{:S(2)}, u32[]{:S(2)}) collective-permute-start(f32[512,256]{1,0:T(8,128)S(1)} %bitcast.10), channel_id=1, source_target_pairs={{0,1},{1,0},{2,3},{3,2},{4,5},{5,4},{6,7},{7,6},{8,9},{9,8},{10,11... | collective-permute-start | bytes 1572872 | tf_op jit(solution)/shard_map/ppermute | solution.py:262
  172.3 6.8 %collective-permute-start.6 = (f32[128,512]{1,0:T(8,128)S(1)}, f32[128,512]{1,0:T(8,128)S(1)}, u32[]{:S(2)}, u32[]{:S(2)}) collective-permute-start(f32[128,512]{1,0:T(8,128)S(1)} %get-tuple-element.37), channel_id=1, source_target_pairs={{0,2},{2,0},{1,3},{3,1},{4,6},{6,4},{5,7},{7,5},{8,10},{10,8},{9,1... | collective-permute-start | bytes 786440 | tf_op jit(solution)/shard_map/ppermute | solution.py:260
